TPU v7x, 256 devices: a whole 4x4x8 slice. The times are simulated.
256 devices in a mesh: gx: 16 (over y, z_hi), gy: 4 (over x), gz: 4 (over z_lo, core).
Axes of the slice: x: 4, y: 4, z: 8 (z_hi: 4, z_lo: 2; z = z_hi * 2 + z_lo), core: 2. Of those that a mesh axis runs over, the one named last changes fastest.
Arguments:
- fields: float32 [6, 256, 64, 512], P(None, 'gx', 'gy', 'gz'), may hold values from -6 to 6
- polarization: float32 [6, 256, 64, 512], P(None, 'gx', 'gy', 'gz'), may hold values from -3 to 3
- material: int32 [256, 64, 512], P('gx', 'gy', 'gz'), may hold values from 0 to 4
- omega0: float32 [4], replicated, may hold values from 0.1 to 0.5
- damping: float32 [4], replicated, may hold values from 0.05 to 0.8
- strength: float32 [4], replicated, may hold values from 0.5 to 2.5
- tile_count: int32 [64, 4], P(('gx', 'gy')), may hold values from 1 to 18, 24 in all within a row
- tile_place: int32 [64, 4, 18], P(('gx', 'gy')), may hold values from 0 to 31, as said below
- dir_angles: float32 [2, 8192], replicated, may hold values from 0 to 3.14159
- dir_order: int32 [8192], replicated, may hold values from 0 to 8191, each once
Outputs:
- fields_out: float32 [6, 256, 64, 512], P(None, 'gx', 'gy', 'gz')
- far_field: float32 [8192, 8], P(('gx', 'gy', 'gz'))
Inputs may be any that keep to these rules, and one draw needn't show every extreme that they name: `tile_count`: for each column g, the 4 counts sum to 24, and the largest of them is exactly 18. `tile_place`: the 18 positions of one device are distinct; only the first tile_count of them are live tiles.
All inputs are finite; a program needn't handle non-finite values.
Results may differ from a plain program's by a relative error of at most 0.0032.
Values may be sent and summed in bfloat16 or wider, within the bound.
No kernel may reach another device: no remote copies, remote signals or barrier semaphores. Data moves between devices by JAX's collectives and lax.ppermute only.
A program may use at most 64 MiB of HBM per device.

v0:
```python
import math

import jax
import jax.numpy as jnp
from jax import lax
from jax.sharding import Mesh
from jax.sharding import PartitionSpec as P

TY = 8
STEPS = 4
DIRS = 8192
TILE_MEAN = 6
GZ = ("gz_0", "gz_1")
GX = ("gx_0", "gx_1")
GX_GY_GZ = ("gx_0", "gx_1", "gy", "gz_0", "gz_1")
GX_GY = ("gx_0", "gx_1", "gy")


SPEED = 0.5
WAVE = 0.35


def with_halo(block, sides, width):
    for axis, dim in sides:
        count = lax.axis_size(axis)
        forward = [(i, i + 1) for i in range(count - 1)]
        backward = [(target, source) for source, target in forward]
        low = lax.ppermute(
            lax.slice_in_dim(block, block.shape[dim] - width, None, axis=dim), axis, forward
        )
        high = lax.ppermute(lax.slice_in_dim(block, 0, width, axis=dim), axis, backward)
        block = jnp.concatenate([low, block, high], axis=dim)
    return block


def in_blocks(array, dim, length):
    before, after = (array.shape[:dim], array.shape[dim + 1 :])
    return jnp.moveaxis(array.reshape(*before, length, -1, *after), dim, 0)


def scatter_pairs(array, chips, core, dim):
    sizes = (lax.axis_size(chips), lax.axis_size(core))
    blocks = in_blocks(array, dim, sizes[0] * sizes[1])
    inside = blocks.shape[1:]
    blocks = blocks.reshape(*sizes, *inside).swapaxes(0, 1).reshape(-1, *inside)
    blocks = lax.psum_scatter(blocks, core, scatter_dimension=0, tiled=True)
    return lax.psum_scatter(blocks, chips, scatter_dimension=0, tiled=True)[0]


def lorentz(omega0, damping, strength):
    denominator = 1.0 + 0.5 * damping
    square = omega0 * omega0
    return (
        (2.0 - square) / denominator,
        -(1.0 - 0.5 * damping) / denominator,
        strength * square / denominator,
    )


def lookup(material, coef_table):
    result = jnp.zeros(material.shape, jnp.float32)
    for mat_index in range(coef_table.shape[0]):
        result = result + jnp.where(material == mat_index + 1, coef_table[mat_index], 0.0)
    return result


def ahead(values, axis_id):
    extent = values.shape[axis_id]
    padded = jnp.pad(
        values, [(0, 1) if other == axis_id else (0, 0) for other in range(values.ndim)]
    )
    return lax.slice_in_dim(padded, 1, extent + 1, axis=axis_id)


def behind(values, axis_id):
    extent = values.shape[axis_id]
    padded = jnp.pad(
        values, [(1, 0) if other == axis_id else (0, 0) for other in range(values.ndim)]
    )
    return lax.slice_in_dim(padded, 0, extent, axis=axis_id)


def magnetic_update(electric, magnetic):
    electric_x, electric_y, electric_z = (electric[0], electric[1], electric[2])
    magnetic_x = magnetic[0] - SPEED * (
        ahead(electric_z, 1) - electric_z - (ahead(electric_y, 2) - electric_y)
    )
    magnetic_y = magnetic[1] - SPEED * (
        ahead(electric_x, 2) - electric_x - (ahead(electric_z, 0) - electric_z)
    )
    magnetic_z = magnetic[2] - SPEED * (
        ahead(electric_y, 0) - electric_y - (ahead(electric_x, 1) - electric_x)
    )
    return jnp.stack([magnetic_x, magnetic_y, magnetic_z])


def curl_back(magnetic):
    magnetic_x, magnetic_y, magnetic_z = (magnetic[0], magnetic[1], magnetic[2])
    curl_x = magnetic_z - behind(magnetic_z, 1) - (magnetic_y - behind(magnetic_y, 2))
    curl_y = magnetic_x - behind(magnetic_x, 2) - (magnetic_z - behind(magnetic_z, 0))
    curl_z = magnetic_y - behind(magnetic_y, 0) - (magnetic_x - behind(magnetic_x, 1))
    return jnp.stack([curl_x, curl_y, curl_z])


def inside_band(offset, extent, total, ghost_depth):
    global_ids = jnp.arange(extent + 2 * ghost_depth) + offset - ghost_depth
    return jnp.where((global_ids >= 0) & (global_ids < total), 1.0, 0.0).astype(jnp.float32)


def tile_patches(values, places, blocks_y):
    width_x, width_y, depth_z = (values.shape[1], values.shape[2], values.shape[3])
    grouped = values.reshape(2, width_x * blocks_y, TY, depth_z)
    return jnp.take(grouped, places, axis=1)


def accumulate(sums, mag_inner, ele_inner, instant, places, blocks_y):
    ele_real, ele_imag, mag_real, mag_imag = sums
    angle_h = WAVE * SPEED * (instant + 0.5)
    angle_e = WAVE * SPEED * (instant + 1.0)
    mag_tiles = tile_patches(mag_inner, places, blocks_y)
    ele_tiles = tile_patches(ele_inner, places, blocks_y)
    mag_real = mag_real + math.cos(angle_h) * mag_tiles
    mag_imag = mag_imag - math.sin(angle_h) * mag_tiles
    ele_real = ele_real + math.cos(angle_e) * ele_tiles
    ele_imag = ele_imag - math.sin(angle_e) * ele_tiles
    return (ele_real, ele_imag, mag_real, mag_imag)


def far_block(currents, tile_x, tile_y, tile_z, directions, rows_y, depth_z):
    row_pos = jnp.arange(rows_y, dtype=jnp.float32)
    depth_pos = jnp.arange(depth_z, dtype=jnp.float32)
    phases = WAVE * (
        directions[1][None, None, :] * row_pos[:, None, None]
        + directions[2][None, None, :] * depth_pos[None, :, None]
    )
    phase_table = jnp.concatenate([jnp.cos(phases), jnp.sin(phases)], axis=2).astype(jnp.bfloat16)
    block_width = directions.shape[1]
    phase_table = phase_table.reshape(rows_y * depth_z, 2 * block_width)
    tiles = currents.shape[0]
    products = jnp.dot(
        currents.reshape(tiles * 8, rows_y * depth_z),
        phase_table,
        preferred_element_type=jnp.float32,
    )
    products = products.reshape(tiles, 4, 2, 2, block_width)
    real_part = products[:, :, 0, 0] - products[:, :, 1, 1]
    imag_part = products[:, :, 0, 1] + products[:, :, 1, 0]
    tile_phase = WAVE * (
        directions[0][None, :] * tile_x[:, None]
        + directions[1][None, :] * tile_y[:, None]
        + directions[2][None, :] * tile_z[:, None]
    )
    tile_cos = jnp.cos(tile_phase)[:, None, :]
    tile_sin = jnp.sin(tile_phase)[:, None, :]
    far_real = jnp.sum(real_part * tile_cos - imag_part * tile_sin, axis=0)
    far_imag = jnp.sum(real_part * tile_sin + imag_part * tile_cos, axis=0)
    return jnp.stack([far_real, far_imag], axis=1).reshape(8, block_width)


def shards(
    fields,
    polarization,
    material,
    omega0,
    damping,
    strength,
    tile_count,
    tile_place,
    dir_angles,
    dir_order,
):
    width_x, width_y, depth_z = (fields.shape[1], fields.shape[2], fields.shape[3])
    blocks_y = width_y // TY
    slot_count = tile_place.shape[2]
    layer_z = lax.axis_index(GZ)
    first_x = lax.axis_index(GX) * width_x
    first_y = lax.axis_index("gy") * width_y
    first_z = layer_z * depth_z
    table_a, table_b, table_c = lorentz(omega0, damping, strength)
    coef_a = lookup(material, table_a)
    coef_b = lookup(material, table_b)
    coef_c = lookup(material, table_c)
    sheet_mask = jnp.where(material > 0, 1.0, 0.0).astype(jnp.float32)
    counts = tile_count[0]
    own_places = lax.dynamic_index_in_dim(tile_place[0], layer_z, 0, keepdims=False)
    empty_sum = jnp.zeros((2, slot_count, TY, depth_z), jnp.float32)
    sums = (empty_sum, empty_sum, empty_sum, empty_sum)
    ghost_depth = STEPS
    stacked = jnp.concatenate(
        [fields, polarization, jnp.stack([coef_a, coef_b, coef_c, sheet_mask])], axis=0
    )
    widened = with_halo(stacked, ((GX, 1), ("gy", 2), (GZ, 3)), STEPS)
    inside = (
        inside_band(first_x, width_x, lax.axis_size(GX) * width_x, ghost_depth)[:, None, None]
        * inside_band(first_y, width_y, lax.axis_size("gy") * width_y, ghost_depth)[None, :, None]
        * inside_band(first_z, depth_z, lax.axis_size(GZ) * depth_z, ghost_depth)[None, None, :]
    )
    electric = widened[0:3]
    magnetic = widened[3:6]
    pol_now = widened[6:9]
    pol_old = widened[9:12]
    wide_a, wide_b, wide_c, wide_sheet = (widened[12], widened[13], widened[14], widened[15])
    for instant in range(STEPS):
        magnetic = magnetic_update(electric, magnetic) * inside[None]
        saturation = 1.0 / (
            1.0 + electric[0] * electric[0] + electric[1] * electric[1] + electric[2] * electric[2]
        )
        pol_new = wide_a * pol_now + wide_b * pol_old + wide_c * saturation * electric
        electric = (
            electric + SPEED * curl_back(magnetic) - wide_sheet * (pol_new - pol_now)
        ) * inside[None]
        pol_old = pol_now
        pol_now = pol_new
        ele_inner = electric[
            :,
            ghost_depth : ghost_depth + width_x,
            ghost_depth : ghost_depth + width_y,
            ghost_depth : ghost_depth + depth_z,
        ]
        mag_inner = magnetic[
            :,
            ghost_depth : ghost_depth + width_x,
            ghost_depth : ghost_depth + width_y,
            ghost_depth : ghost_depth + depth_z,
        ]
        sums = accumulate(sums, mag_inner[1:3], ele_inner[1:3], instant, own_places, blocks_y)
    field_state = jnp.concatenate([ele_inner, mag_inner], axis=0)
    ele_real, ele_imag, mag_real, mag_imag = sums
    currents = jnp.stack(
        [
            -mag_real[1],
            -mag_imag[1],
            mag_real[0],
            mag_imag[0],
            ele_real[1],
            ele_imag[1],
            -ele_real[0],
            -ele_imag[0],
        ],
        axis=1,
    )
    live_mask = (jnp.arange(slot_count) < counts[layer_z]).astype(jnp.float32)
    currents = (
        (currents * live_mask[:, None, None, None])
        .reshape(slot_count, 8, TY * depth_z)
        .astype(jnp.bfloat16)
    )
    chosen = currents
    tile_z = jnp.zeros((slot_count,), jnp.float32) + first_z.astype(jnp.float32)
    tile_x = (first_x + own_places // blocks_y).astype(jnp.float32)
    tile_y = (first_y + own_places % blocks_y * TY).astype(jnp.float32)
    polar_angle = jnp.take(dir_angles[0], dir_order)
    azimuth = jnp.take(dir_angles[1], dir_order)
    dir_vec = jnp.stack(
        [
            jnp.sin(polar_angle) * jnp.cos(azimuth),
            jnp.sin(polar_angle) * jnp.sin(azimuth),
            jnp.cos(polar_angle),
        ]
    )
    tile_total = lax.axis_size(GX) * lax.axis_size("gy") * lax.axis_size(GZ) * TILE_MEAN
    norm_scale = 1.0 / math.sqrt(tile_total * TY * depth_z)
    devices_all = lax.axis_size(GX_GY_GZ)
    block_width = math.gcd(
        DIRS // devices_all * lax.axis_size(("gx_0", "gx_1", "gy", "gz_0")) * lax.axis_size("gz_1"),
        512,
    )

    def block_far(offset):
        directions = lax.dynamic_slice_in_dim(dir_vec, offset, block_width, 1)
        return far_block(chosen, tile_x, tile_y, tile_z, directions, TY, depth_z)

    far_blocks = lax.map(
        block_far,
        jnp.arange(
            DIRS
            // devices_all
            * lax.axis_size(("gx_0", "gx_1", "gy", "gz_0"))
            * lax.axis_size("gz_1")
            // block_width,
            dtype=jnp.int32,
        )
        * block_width,
    )
    far_field = scatter_pairs(
        far_blocks.transpose(0, 2, 1).reshape(
            DIRS
            // devices_all
            * lax.axis_size(("gx_0", "gx_1", "gy", "gz_0"))
            * lax.axis_size("gz_1"),
            8,
        )
        * norm_scale,
        ("gx_0", "gx_1", "gy", "gz_0"),
        "gz_1",
        0,
    )
    return (field_state, far_field)


def solution(mesh):
    torus = Mesh(
        mesh.devices.reshape(4, 4, mesh.shape["gy"], 2, 2), ("gx_0", "gx_1", "gy", "gz_0", "gz_1")
    )
    return jax.shard_map(
        shards,
        mesh=torus,
        in_specs=(
            P(None, GX, "gy", GZ),
            P(None, GX, "gy", GZ),
            P(GX, "gy", GZ),
            P(),
            P(),
            P(),
            P(GX_GY, None),
            P(GX_GY, None, None),
            P(),
            P(),
        ),
        out_specs=(P(None, GX, "gy", GZ), P(GX_GY_GZ, None)),
        check_vma=False,
    )
```

profile of v0, /device:TPU:1, one launch (start us, length us, event | category | flops | bytes accessed | tf_op | source)
XLA Modules:
  0.0 693.5 jit_solution(8837939853066778752)
XLA Ops:
  10.7 2.6 bitcast_dynamic-update-slice_fusion.3
  13.3 2.6 bitcast_dynamic-update-slice_fusion.2
  15.9 2.6 bitcast_dynamic-update-slice_fusion.1
  20.9 7.2 %collective-permute-start = (f32[16,4,16,128]{3,2,1,0:T(8,128)}, f32[16,4,16,128]{3,2,1,0:T(8,128)}, u32[]{:S(2)}, u32[]{:S(2)}) collective-permute-start(f32[16,4,16,128]{3,2,1,0:T(8,128)} %get-tuple-element.130), channel_id=1, source_target_pairs={{0,16},{16,32},{32,48},{48,64},{64,80},{80,96},{96,112},{112,128},... | collective-permute-start | bytes 1572872 | tf_op jit(solution)/shard_map/ppermute | solution.py:28
  28.2 45.5 %gather_fusion.1 = f32[8192]{0:T(1024)S(1)} fusion(f32[8192]{0:T(1024)S(1)} %bitcast.333, s32[8192]{0:T(1024)S(1)} %fusion.150), kind=kCustom, calls=%fused_computation.2.clone | custom fusion | bytes 98304 | tf_op jit(solution)/shard_map/jit(_take)/gather | solution.py:253
  73.7 45.5 %gather_fusion = f32[8192]{0:T(1024)S(1)} fusion(f32[8192]{0:T(1024)S(1)} %bitcast.332, s32[8192]{0:T(1024)S(1)} %fusion.150), kind=kCustom, calls=%fused_computation.clone | custom fusion | bytes 98304 | tf_op jit(solution)/shard_map/jit(_take)/gather | solution.py:252
  121.4 1.6 pad_maximum_fusion.6
  124.3 4.9 collective-permute-start.2
  129.9 11.8 %collective-permute-done.3 = f32[16,24,4,128]{3,2,1,0:T(4,128)S(1)} collective-permute-done((f32[16,24,4,128]{3,2,1,0:T(4,128)S(1)}, f32[16,24,4,128]{3,2,1,0:T(4,128)S(1)}, u32[]{:S(2)}, u32[]{:S(2)}) %collective-permute-start.3) | collective-permute-done | bytes 786464 | tf_op jit(solution)/shard_map/ppermute | solution.py:31
  142.6 2.1 pad_maximum_fusion.2
  144.7 5.3 fusion.156
  150.1 4.9 copy.69
  154.9 5.3 collective-permute-start.5
  160.3 4.9 copy.68
  165.2 3.6 collective-permute-start.4
  169.5 2.3 collective-permute-done.5
  171.8 4.8 copy.71
  177.8 4.9 copy.70
  182.8 3.3 multiply_bitcast_fusion.3
  189.9 1.4 fusion.100
  192.1 9.3 %pad_maximum_fusion.1 = f32[16,24,24,136]{3,2,1,0:T(8,128)S(1)} fusion(f32[16,24,24,4]{3,2,1,0:T(8,128)S(1)} %bitcast.335, f32[16,24,4,128]{3,2,1,0:T(4,128)S(1)} %collective-permute-done.3, f32[16,4,16,128]{3,2,1,0:T(8,128)S(1)} %copy-done.4, f32[16,16,16,128]{3,2,1,0:T(8,128)S(1)} %bitcast_dynamic-update-slice_fusion, ...), kind=kLoop, calls=%fused_computation.39 | loop fusion | flops 7520256 | bytes 10027008 | tf_op jit(solution)/shard_map/concatenate | solution.py:32
  201.4 1.6 maximum_bitcast_fusion.1
  204.2 5.3 fusion.22
  219.6 2.1 fusion.31
  223.8 2.2 gather_fusion.9
  229.0 1.5 gather_fusion.5
  235.3 208.8 %while.11 = (s32[]{:T(128)}, f32[16,8,512]{2,1,0:T(8,128)S(1)}, s32[16]{0:T(128)S(1)}, f32[3,8192]{1,0:T(4,128)}, bf16[18,8,1024]{2,1,0:T(8,128)(2,1)S(1)}, /*in...) while((s32[]{:T(128)}, f32[16,8,512]{2,1,0:T(8,128)S(1)}, ...), condition=%wide.region_3.6_spmd.clone, body=%wide.region_0.5_spmd.clone.sunk | while | flops 308766208 | bytes 8612207 | solution.py:273
  238.8 7.7 %cosine_convert_fusion.2 = (bf16[8,128,512]{2,1,0:T(8,128)(2,1)S(1)}, bf16[8,128,512]{2,1,0:T(8,128)(2,1)S(1)}) fusion(f32[128,512]{1,0:T(8,128)S(1)} %iota_multiply_fusion.5, f32[8,512]{1,0:T(8,128)S(1)} %iota_multiply_fusion.6), kind=kLoop, calls=%fused_computation.16.clone.1 | loop fusion | flops 2097152 | bytes 2375680 | tf_op jit(solution)/shard_map/convert.3
  251.9 7.7 %cosine_convert_fusion.2 = (bf16[8,128,512]{2,1,0:T(8,128)(2,1)S(1)}, bf16[8,128,512]{2,1,0:T(8,128)(2,1)S(1)}) fusion(f32[128,512]{1,0:T(8,128)S(1)} %iota_multiply_fusion.5, f32[8,512]{1,0:T(8,128)S(1)} %iota_multiply_fusion.6), kind=kLoop, calls=%fused_computation.16.clone.1 | loop fusion | flops 2097152 | bytes 2375680 | tf_op jit(solution)/shard_map/convert.3
  264.9 7.7 %cosine_convert_fusion.2 = (bf16[8,128,512]{2,1,0:T(8,128)(2,1)S(1)}, bf16[8,128,512]{2,1,0:T(8,128)(2,1)S(1)}) fusion(f32[128,512]{1,0:T(8,128)S(1)} %iota_multiply_fusion.5, f32[8,512]{1,0:T(8,128)S(1)} %iota_multiply_fusion.6), kind=kLoop, calls=%fused_computation.16.clone.1 | loop fusion | flops 2097152 | bytes 2375680 | tf_op jit(solution)/shard_map/convert.3
  278.0 7.7 %cosine_convert_fusion.2 = (bf16[8,128,512]{2,1,0:T(8,128)(2,1)S(1)}, bf16[8,128,512]{2,1,0:T(8,128)(2,1)S(1)}) fusion(f32[128,512]{1,0:T(8,128)S(1)} %iota_multiply_fusion.5, f32[8,512]{1,0:T(8,128)S(1)} %iota_multiply_fusion.6), kind=kLoop, calls=%fused_computation.16.clone.1 | loop fusion | flops 2097152 | bytes 2375680 | tf_op jit(solution)/shard_map/convert.3
  291.0 7.7 %cosine_convert_fusion.2 = (bf16[8,128,512]{2,1,0:T(8,128)(2,1)S(1)}, bf16[8,128,512]{2,1,0:T(8,128)(2,1)S(1)}) fusion(f32[128,512]{1,0:T(8,128)S(1)} %iota_multiply_fusion.5, f32[8,512]{1,0:T(8,128)S(1)} %iota_multiply_fusion.6), kind=kLoop, calls=%fused_computation.16.clone.1 | loop fusion | flops 2097152 | bytes 2375680 | tf_op jit(solution)/shard_map/convert.3
  304.1 7.7 %cosine_convert_fusion.2 = (bf16[8,128,512]{2,1,0:T(8,128)(2,1)S(1)}, bf16[8,128,512]{2,1,0:T(8,128)(2,1)S(1)}) fusion(f32[128,512]{1,0:T(8,128)S(1)} %iota_multiply_fusion.5, f32[8,512]{1,0:T(8,128)S(1)} %iota_multiply_fusion.6), kind=kLoop, calls=%fused_computation.16.clone.1 | loop fusion | flops 2097152 | bytes 2375680 | tf_op jit(solution)/shard_map/convert.3
  317.1 7.7 %cosine_convert_fusion.2 = (bf16[8,128,512]{2,1,0:T(8,128)(2,1)S(1)}, bf16[8,128,512]{2,1,0:T(8,128)(2,1)S(1)}) fusion(f32[128,512]{1,0:T(8,128)S(1)} %iota_multiply_fusion.5, f32[8,512]{1,0:T(8,128)S(1)} %iota_multiply_fusion.6), kind=kLoop, calls=%fused_computation.16.clone.1 | loop fusion | flops 2097152 | bytes 2375680 | tf_op jit(solution)/shard_map/convert.3
  330.2 7.7 %cosine_convert_fusion.2 = (bf16[8,128,512]{2,1,0:T(8,128)(2,1)S(1)}, bf16[8,128,512]{2,1,0:T(8,128)(2,1)S(1)}) fusion(f32[128,512]{1,0:T(8,128)S(1)} %iota_multiply_fusion.5, f32[8,512]{1,0:T(8,128)S(1)} %iota_multiply_fusion.6), kind=kLoop, calls=%fused_computation.16.clone.1 | loop fusion | flops 2097152 | bytes 2375680 | tf_op jit(solution)/shard_map/convert.3
  343.2 7.7 %cosine_convert_fusion.2 = (bf16[8,128,512]{2,1,0:T(8,128)(2,1)S(1)}, bf16[8,128,512]{2,1,0:T(8,128)(2,1)S(1)}) fusion(f32[128,512]{1,0:T(8,128)S(1)} %iota_multiply_fusion.5, f32[8,512]{1,0:T(8,128)S(1)} %iota_multiply_fusion.6), kind=kLoop, calls=%fused_computation.16.clone.1 | loop fusion | flops 2097152 | bytes 2375680 | tf_op jit(solution)/shard_map/convert.3
  356.3 7.7 %cosine_convert_fusion.2 = (bf16[8,128,512]{2,1,0:T(8,128)(2,1)S(1)}, bf16[8,128,512]{2,1,0:T(8,128)(2,1)S(1)}) fusion(f32[128,512]{1,0:T(8,128)S(1)} %iota_multiply_fusion.5, f32[8,512]{1,0:T(8,128)S(1)} %iota_multiply_fusion.6), kind=kLoop, calls=%fused_computation.16.clone.1 | loop fusion | flops 2097152 | bytes 2375680 | tf_op jit(solution)/shard_map/convert.3
  369.4 7.7 %cosine_convert_fusion.2 = (bf16[8,128,512]{2,1,0:T(8,128)(2,1)S(1)}, bf16[8,128,512]{2,1,0:T(8,128)(2,1)S(1)}) fusion(f32[128,512]{1,0:T(8,128)S(1)} %iota_multiply_fusion.5, f32[8,512]{1,0:T(8,128)S(1)} %iota_multiply_fusion.6), kind=kLoop, calls=%fused_computation.16.clone.1 | loop fusion | flops 2097152 | bytes 2375680 | tf_op jit(solution)/shard_map/convert.3
  382.4 7.7 %cosine_convert_fusion.2 = (bf16[8,128,512]{2,1,0:T(8,128)(2,1)S(1)}, bf16[8,128,512]{2,1,0:T(8,128)(2,1)S(1)}) fusion(f32[128,512]{1,0:T(8,128)S(1)} %iota_multiply_fusion.5, f32[8,512]{1,0:T(8,128)S(1)} %iota_multiply_fusion.6), kind=kLoop, calls=%fused_computation.16.clone.1 | loop fusion | flops 2097152 | bytes 2375680 | tf_op jit(solution)/shard_map/convert.3
  395.5 7.7 %cosine_convert_fusion.2 = (bf16[8,128,512]{2,1,0:T(8,128)(2,1)S(1)}, bf16[8,128,512]{2,1,0:T(8,128)(2,1)S(1)}) fusion(f32[128,512]{1,0:T(8,128)S(1)} %iota_multiply_fusion.5, f32[8,512]{1,0:T(8,128)S(1)} %iota_multiply_fusion.6), kind=kLoop, calls=%fused_computation.16.clone.1 | loop fusion | flops 2097152 | bytes 2375680 | tf_op jit(solution)/shard_map/convert.3
  408.5 7.7 %cosine_convert_fusion.2 = (bf16[8,128,512]{2,1,0:T(8,128)(2,1)S(1)}, bf16[8,128,512]{2,1,0:T(8,128)(2,1)S(1)}) fusion(f32[128,512]{1,0:T(8,128)S(1)} %iota_multiply_fusion.5, f32[8,512]{1,0:T(8,128)S(1)} %iota_multiply_fusion.6), kind=kLoop, calls=%fused_computation.16.clone.1 | loop fusion | flops 2097152 | bytes 2375680 | tf_op jit(solution)/shard_map/convert.3
  421.6 7.7 %cosine_convert_fusion.2 = (bf16[8,128,512]{2,1,0:T(8,128)(2,1)S(1)}, bf16[8,128,512]{2,1,0:T(8,128)(2,1)S(1)}) fusion(f32[128,512]{1,0:T(8,128)S(1)} %iota_multiply_fusion.5, f32[8,512]{1,0:T(8,128)S(1)} %iota_multiply_fusion.6), kind=kLoop, calls=%fused_computation.16.clone.1 | loop fusion | flops 2097152 | bytes 2375680 | tf_op jit(solution)/shard_map/convert.3
  434.6 7.7 %cosine_convert_fusion.2 = (bf16[8,128,512]{2,1,0:T(8,128)(2,1)S(1)}, bf16[8,128,512]{2,1,0:T(8,128)(2,1)S(1)}) fusion(f32[128,512]{1,0:T(8,128)S(1)} %iota_multiply_fusion.5, f32[8,512]{1,0:T(8,128)S(1)} %iota_multiply_fusion.6), kind=kLoop, calls=%fused_computation.16.clone.1 | loop fusion | flops 2097152 | bytes 2375680 | tf_op jit(solution)/shard_map/convert.3
  447.6 1.4 slice.617
  449.0 15.5 %reduce-scatter.2.cloned.1.call-done = f32[128,32,8]{0,2,1:T(8,128)} async-done(((f32[256,32,8]{0,2,1:T(8,128)}), f32[128,32,8]{0,2,1:T(8,128)}) %reduce-scatter.2.cloned.1.call-update) | async-done | bytes 131088 | tf_op jit(solution)/shard_map/reduce_scatter | solution.py:46
  464.5 1.9 copy.74
  467.4 217.5 %all-reduce.51.cloned.1.call-done = f32[128,32,8]{1,2,0:T(8,128)} async-done(((f32[128,32,8]{1,2,0:T(8,128)}), f32[128,32,8]{1,2,0:T(8,128)}) %all-reduce.51.cloned.1.call-update) | async-done | bytes 131088
  684.9 1.8 dynamic-slice_bitcast_fusion
  (366 shorter events, 96.0 us)
Async XLA Ops:
  7.2 112.1 %copy-start = (s32[1,4]{1,0:T(1,128)S(1)}, s32[1,4]{1,0:T(1,128)}, u32[]{:S(2)}) copy-start(s32[1,4]{1,0:T(1,128)} %param.22) | copy-start | bytes 52
  7.2 2.7 copy-start.7
  7.2 3.5 copy-start.12
  7.2 457.3 %reduce-scatter.2.cloned.1.call-start = ((), (), s32[]{:S(2)}) async-start(), calls=%async_computation.1 | async-start | bytes 393216 | tf_op jit(solution)/shard_map/reduce_scatter | solution.py:46
  10.0 18.1 %copy-start.16 = (s32[1,4,18]{2,1,0:T(4,128)S(1)}, s32[1,4,18]{2,1,0:T(4,128)}, u32[]{:S(2)}) copy-start(s32[1,4,18]{2,1,0:T(4,128)} %param.23) | copy-start | bytes 868
  10.0 18.1 %copy-start.15 = (f32[2,8192]{1,0:T(2,128)S(1)}, f32[2,8192]{1,0:T(2,128)}, u32[]{:S(2)}) copy-start(f32[2,8192]{1,0:T(2,128)} %param.24) | copy-start | bytes 196612
  10.0 18.2 %copy-start.14 = (s32[8192]{0:T(1024)S(1)}, s32[8192]{0:T(1024)}, u32[]{:S(2)}) copy-start(s32[8192]{0:T(1024)} %param.25) | copy-start | bytes 98308
  19.6 101.8 %collective-permute-start.1 = (f32[16,4,16,128]{3,2,1,0:T(8,128)}, f32[16,4,16,128]{3,2,1,0:T(8,128)S(1)}, u32[]{:S(2)}, u32[]{:S(2)}) collective-permute-start(f32[16,4,16,128]{3,2,1,0:T(8,128)} %get-tuple-element.131), channel_id=1, source_target_pairs={{16,0},{32,16},{48,32},{64,48},{80,64},{96,80},{112,96},{128,112},... | collective-permute-start | bytes 1572872 | tf_op jit(solution)/shard_map/ppermute | solution.py:31
  20.9 100.5 %collective-permute-start = (f32[16,4,16,128]{3,2,1,0:T(8,128)}, f32[16,4,16,128]{3,2,1,0:T(8,128)}, u32[]{:S(2)}, u32[]{:S(2)}) collective-permute-start(f32[16,4,16,128]{3,2,1,0:T(8,128)} %get-tuple-element.130), channel_id=1, source_target_pairs={{0,16},{16,32},{32,48},{48,64},{64,80},{80,96},{96,112},{112,128},... | collective-permute-start | bytes 1572872 | tf_op jit(solution)/shard_map/ppermute | solution.py:28
  121.4 1.6 copy-start.3
  123.0 18.7 %collective-permute-start.3 = (f32[16,24,4,128]{3,2,1,0:T(4,128)S(1)}, f32[16,24,4,128]{3,2,1,0:T(4,128)S(1)}, u32[]{:S(2)}, u32[]{:S(2)}) collective-permute-start(f32[16,24,4,128]{3,2,1,0:T(4,128)S(1)} %get-tuple-element.120), channel_id=1, source_target_pairs={{4,0},{8,4},{12,8},{5,1},{9,5},{13,9},{6,2},{10,6},{14,10},{7,3},{... | collective-permute-start | bytes 2359304 | tf_op jit(solution)/shard_map/ppermute | solution.py:31
  124.3 18.3 %collective-permute-start.2 = (f32[16,24,4,128]{3,2,1,0:T(4,128)S(1)}, f32[16,24,4,128]{3,2,1,0:T(4,128)}, u32[]{:S(2)}, u32[]{:S(2)}) collective-permute-start(f32[16,24,4,128]{3,2,1,0:T(4,128)S(1)} %get-tuple-element.119), channel_id=1, source_target_pairs={{0,4},{4,8},{8,12},{1,5},{5,9},{9,13},{2,6},{6,10},{10,14},{3,7},{... | collective-permute-start | bytes 2359304 | tf_op jit(solution)/shard_map/ppermute | solution.py:28
  154.9 16.8 %collective-permute-start.5 = (f32[16,24,24,4]{2,1,3,0:T(8,128)}, f32[16,24,24,4]{2,1,3,0:T(8,128)}, u32[]{:S(2)}, u32[]{:S(2)}) collective-permute-start(f32[16,24,24,4]{2,1,3,0:T(8,128)} %copy.69), channel_id=1, source_target_pairs={{1,0},{2,1},{3,2},{5,4},{6,5},{7,6},{9,8},{10,9},{11,10},{13,12},{... | collective-permute-start | bytes 442376 | tf_op jit(solution)/shard_map/ppermute | solution.py:31
  165.2 12.7 %collective-permute-start.4 = (f32[16,24,24,4]{2,1,3,0:T(8,128)}, f32[16,24,24,4]{2,1,3,0:T(8,128)}, u32[]{:S(2)}, u32[]{:S(2)}) collective-permute-start(f32[16,24,24,4]{2,1,3,0:T(8,128)} %copy.68), channel_id=1, source_target_pairs={{0,1},{1,2},{2,3},{4,5},{5,6},{6,7},{8,9},{9,10},{10,11},{12,13},{... | collective-permute-start | bytes 442376 | tf_op jit(solution)/shard_map/ppermute | solution.py:28
  177.8 8.2 %slice-start = ((s8[4718592]{0:T(1024)(128)(4,1)}), s8[524288]{0:T(1024)(128)(4,1)S(1)}, s32[]{:S(2)}) async-start(s8[4718592]{0:T(1024)(128)(4,1)} %bitcast.334), calls=%async_computation.3 | async-start | bytes 1048576
  182.8 3.3 slice-start.1
  182.8 4.5 copy-start.2
  182.8 4.5 copy-start.4
  189.9 1.5 copy-start.5
  221.7 1.3 copy-start.6
  222.9 7.6 %copy-start.8 = (f32[2,16,16,128]{3,2,1,0:T(8,128)S(1)}, f32[2,16,16,128]{3,2,1,0:T(8,128)}, u32[]{:S(2)}) copy-start(f32[2,16,16,128]{3,2,1,0:T(8,128)} %slice.621) | copy-start | bytes 786436
  222.9 8.8 %copy-start.9 = (f32[2,16,16,128]{3,2,1,0:T(8,128)S(1)}, f32[2,16,16,128]{3,2,1,0:T(8,128)}, u32[]{:S(2)}) copy-start(f32[2,16,16,128]{3,2,1,0:T(8,128)} %slice.620) | copy-start | bytes 786436
  227.2 5.7 copy-start.10
  227.2 5.7 copy-start.11
  234.2 1.1 copy-start.13
  444.4 2.4 copy-start.17
  446.7 238.1 %all-reduce.51.cloned.1.call-start = ((), (), s32[]{:S(2)}) async-start(), calls=%async_computation.2 | async-start | bytes 1048576
  447.4 239.3 %copy-start.1 = (s32[1,4]{1,0:T(1,128)S(1)}, s32[1,4]{1,0:T(1,128)}, u32[]{:S(2)}) copy-start(s32[1,4]{1,0:T(1,128)} %param.22) | copy-start | bytes 52
Sparse Core Ops, SparseCore 0:
  446.9 17.5 reduce-scatter.1
  469.9 214.9 all-reduce.50
where the time goes:
time: 700 us; the launch traced here: 694 us
  waiting for transfers between devices  249 us (36%)
  other arithmetic  187 us (27%)
  local copies, waits for them, and re-layouts  178 us (25%)
  loops' own time  32.8 us (5%)
  starting transfers between devices  23.6 us (3%)
  between operations  14.8 us (2%)
  matrix products  7.62 us (1%)
    unnamed x3, waiting for transfers between devices  218 us
    another operation x16, other arithmetic  123 us
    gather x1, local copies, waits for them, and re-layouts, shards(): polar_angle = jnp.take(dir_angles[0], dir_order)  45.5 us
    gather x1, local copies, waits for them, and re-layouts, shards(): azimuth = jnp.take(dir_angles[1], dir_order)  45.5 us
    another operation x1, loops' own time, shards(): lax.map(block_far, jnp.arange(DIRS // devices_all * lax.axis_size(('gx_0'...  32.8 us
    ppermute x3, starting transfers between devices, with_halo(): lax.ppermute(lax.slice_in_dim(block, block.shape[dim] - width, None, axis...  15.7 us
    reduce_scatter x1, waiting for transfers between devices, scatter_pairs(): blocks = lax.psum_scatter(blocks, core, scatter_dimension=0, tiled=True)  15.5 us
    slice x16, local copies, waits for them, and re-layouts, far_block(): directions[0][None, :] * tile_x[:, None]  14.4 us
  transfers between devices with their start and end apart: 8, of which 6 were waited for; matrix products, arithmetic and copies ran while one was open for 16% of the time, Pallas kernels for 0%

commit v1 on v0

v1 whole, which is shorter than its diff:
```python
import functools
import math

import jax
import jax.numpy as jnp
from jax import lax
from jax.experimental import pallas as pl
from jax.experimental.pallas import tpu as pltpu
from jax.sharding import PartitionSpec as P

TY = 8
STEPS = 4
TILE_MEAN = 6
SLOTS = 18
SPEED = 0.5
WAVE = 0.35
HALO = jnp.bfloat16
AXES = ("gx", "gy", "gz")


def whole():
    return pl.BlockSpec(memory_space=pltpu.VMEM)


def scalars():
    return pl.BlockSpec(memory_space=pltpu.SMEM)


def pack_depth_kernel(fields_ref, pol_ref, mat_ref, out_ref):
    lane = lax.broadcasted_iota(jnp.int32, (16, 128), 1) // 8

    def packed(plane):
        acc = jnp.zeros((16, 128), jnp.float32)
        for x in range(16):
            acc = jnp.where(lane == x, pltpu.roll(plane(x), (8 * x + 4) % 128, 1), acc)
        return acc.astype(HALO)

    def body(a, carry):
        out_ref[a] = packed(lambda x: fields_ref[a, x])
        out_ref[a + 6] = packed(lambda x: pol_ref[a, x])
        return carry

    lax.fori_loop(0, 6, body, 0)
    out_ref[12] = packed(lambda x: mat_ref[x].astype(jnp.float32))


def join_depth(before, after):
    lane = lax.broadcasted_iota(jnp.int32, (16, 128), 1) % 8
    return jnp.where(lane < 4, before.astype(jnp.float32), after.astype(jnp.float32))


def pack_x_kernel(fields_ref, pol_ref, mat_ref, before_ref, after_ref, low_ref, high_ref):
    def put(a, plane):
        for k in range(4):
            low_ref[a, k] = plane(k).astype(HALO)
            high_ref[a, k] = plane(12 + k).astype(HALO)
        depth = join_depth(before_ref[a], after_ref[a]).astype(HALO)
        low_ref[a, 4] = depth
        high_ref[a, 4] = depth

    def body(a, carry):
        put(a, lambda x: fields_ref[a, x])
        put(a + 6, lambda x: pol_ref[a, x])
        return carry

    lax.fori_loop(0, 6, body, 0)
    put(12, lambda x: mat_ref[x].astype(jnp.float32))


def wide_plane(x, a, plane, before_ref, after_ref, left_ref, right_ref):
    if x < 16:
        return plane(x)
    if x < 20:
        return right_ref[a, x - 16].astype(jnp.float32)
    if x < 24:
        return left_ref[a, x - 20].astype(jnp.float32)
    if x == 24:
        return join_depth(before_ref[a], after_ref[a])
    lane = lax.broadcasted_iota(jnp.int32, (16, 128), 1)
    return jnp.where(
        lane < 32,
        right_ref[a, 4].astype(jnp.float32),
        pltpu.roll(left_ref[a, 4].astype(jnp.float32), 64, 1),
    )


def pack_y_kernel(
    fields_ref, pol_ref, mat_ref, before_ref, after_ref, left_ref, right_ref, low_ref, high_ref
):
    top = lax.broadcasted_iota(jnp.int32, (8, 128), 0) < 4

    def put(a, plane):
        for i in range(13):
            p0, p1 = [
                wide_plane(2 * i + k, a, plane, before_ref, after_ref, left_ref, right_ref)
                for k in range(2)
            ]
            low_ref[a, i] = jnp.where(top, p0[0:8], pltpu.roll(p1[0:8], 4, 0)).astype(HALO)
            high_ref[a, i] = jnp.where(top, pltpu.roll(p1[8:16], 4, 0), p0[8:16]).astype(HALO)

    def body(a, carry):
        put(a, lambda x: fields_ref[a, x])
        put(a + 6, lambda x: pol_ref[a, x])
        return carry

    lax.fori_loop(0, 6, body, 0)
    put(12, lambda x: mat_ref[x].astype(jnp.float32))


def window_kernel(
    extents,
    place_ref,
    count_ref,
    index_ref,
    omega_ref,
    damping_ref,
    strength_ref,
    fields_ref,
    pol_ref,
    mat_ref,
    before_ref,
    after_ref,
    left_ref,
    right_ref,
    down_ref,
    up_ref,
    out_ref,
    cur_ref,
    wide_ref,
    coef_ref,
    phasor_ref,
):
    top = lax.broadcasted_iota(jnp.int32, (8, 128), 0) < 4

    def spread(a, plane, store):
        def rows(i):
            lowest = up_ref[a, i].astype(jnp.float32)
            highest = down_ref[a, i].astype(jnp.float32)
            return (
                jnp.where(top, lowest, highest),
                pltpu.roll(jnp.where(top, highest, lowest), 4, 0),
            )

        depth = []
        tail = rows(12)
        for k in range(2):
            body = wide_plane(24 + k, a, plane, before_ref, after_ref, left_ref, right_ref)
            depth.append(jnp.concatenate([body, tail[k]], axis=0))
        for i in range(12):
            tail = rows(i)
            for k in range(2):
                x = 2 * i + k
                body = wide_plane(x, a, plane, before_ref, after_ref, left_ref, right_ref)
                main = jnp.concatenate([body, tail[k]], axis=0)
                side = pltpu.roll(depth[x // 16], (124 - 8 * x) % 128, 1)
                store(x, jnp.concatenate([main, side], axis=1))

    def store_wide(a):
        def store(x, value):
            wide_ref[a, x] = value

        return store

    def body(a, carry):
        spread(a, lambda x: fields_ref[a, x], store_wide(a))
        spread(a + 6, lambda x: pol_ref[a, x], store_wide(a + 6))
        return carry

    lax.fori_loop(0, 6, body, 0)

    table_a, table_b, table_c = [], [], []
    for m in range(4):
        omega, damp, strong = omega_ref[m], damping_ref[m], strength_ref[m]
        full = jnp.full((8, 256), omega, jnp.float32)
        square = full * full
        half = 0.5 * jnp.full((8, 256), damp, jnp.float32)
        under = 1.0 + half
        table_a.append(((2.0 - square) / under)[0:1])
        table_b.append((-(1.0 - half) / under)[0:1])
        table_c.append((jnp.full((8, 256), strong, jnp.float32) * square / under)[0:1])

    def store_coef(x, value):
        a = jnp.zeros((24, 256), jnp.float32)
        b, c = a, a
        for m in range(4):
            hit = value == float(m + 1)
            a = jnp.where(hit, table_a[m], a)
            b = jnp.where(hit, table_b[m], b)
            c = jnp.where(hit, table_c[m], c)
        coef_ref[0, x] = a
        coef_ref[1, x] = b
        coef_ref[2, x] = c
        coef_ref[3, x] = jnp.where(value > 0.0, 1.0, 0.0)

    spread(12, lambda x: mat_ref[x].astype(jnp.float32), store_coef)

    gx, gy, gz = index_ref[0], index_ref[1], index_ref[2]
    row = lax.broadcasted_iota(jnp.int32, (24, 256), 0)
    row = jnp.where(row < 20, row, row - 24) + gy * 16
    lane = lax.broadcasted_iota(jnp.int32, (24, 256), 1)
    near = (lane < 132) | (lane >= 252)
    lane = jnp.where(lane < 132, lane, lane - 256) + gz * 128
    inside = near & (row >= 0) & (row < extents[1]) & (lane >= 0) & (lane < extents[2])
    inside = jnp.where(inside, SPEED, 0.0).astype(jnp.float32)
    phasor_ref[...] = jnp.zeros_like(phasor_ref)

    def ahead_y(v):
        return pltpu.roll(v, 23, 0)

    def behind_y(v):
        return pltpu.roll(v, 1, 0)

    def ahead_z(v):
        return pltpu.roll(v, 255, 1)

    def behind_z(v):
        return pltpu.roll(v, 1, 1)

    def plane_step(n, x, inner):
        here = jnp.where(x < 0, x + 24, x)
        after = jnp.where(x + 1 < 0, x + 25, x + 1)
        prior = jnp.where(x < 1, x + 23, x - 1)
        place = gx * 16 + x
        speed = inside * jnp.where((place >= 0) & (place < extents[0]), 1.0, 0.0)
        ex, ey, ez = wide_ref[0, here], wide_ref[1, here], wide_ref[2, here]
        ey_next, ez_next = wide_ref[1, after], wide_ref[2, after]
        hx = wide_ref[3, here] - speed * ((ahead_y(ez) - ez) - (ahead_z(ey) - ey))
        hy = wide_ref[4, here] - speed * ((ahead_z(ex) - ex) - (ez_next - ez))
        hz = wide_ref[5, here] - speed * ((ey_next - ey) - (ahead_y(ex) - ex))
        wide_ref[3, here] = hx
        wide_ref[4, here] = hy
        wide_ref[5, here] = hz
        hy_prior, hz_prior = wide_ref[4, prior], wide_ref[5, prior]
        sat = 1.0 / (1.0 + ex * ex + ey * ey + ez * ez)
        a, b, sheet = coef_ref[0, here], coef_ref[1, here], coef_ref[3, here]
        drive = coef_ref[2, here] * sat
        now, old = (6, 9) if n % 2 == 0 else (9, 6)
        curls = (
            (hz - behind_y(hz)) - (hy - behind_z(hy)),
            (hx - behind_z(hx)) - (hz - hz_prior),
            (hy - hy_prior) - (hx - behind_y(hx)),
        )
        fresh = []
        for c, e in enumerate((ex, ey, ez)):
            pol = wide_ref[now + c, here]
            pol_new = a * pol + b * wide_ref[old + c, here] + drive * e
            wide_ref[old + c, here] = pol_new
            value = e + speed * curls[c] - sheet * (pol_new - pol)
            wide_ref[c, here] = value
            fresh.append(value)
        if inner:
            angle_h = WAVE * SPEED * (n + 0.5)
            angle_e = WAVE * SPEED * (n + 1.0)
            hy, hz = hy[0:16, 0:128], hz[0:16, 0:128]
            ey, ez = fresh[1][0:16, 0:128], fresh[2][0:16, 0:128]
            terms = (
                (-math.cos(angle_h), hz),
                (math.cos(angle_h), hy),
                (math.cos(angle_e), ez),
                (-math.cos(angle_e), ey),
                (math.sin(angle_h), hz),
                (-math.sin(angle_h), hy),
                (-math.sin(angle_e), ez),
                (math.sin(angle_e), ey),
            )
            for o, (factor, value) in enumerate(terms):
                phasor_ref[o, x] = phasor_ref[o, x] + factor * value
            if n == STEPS - 1:
                for c in range(3):
                    out_ref[c, x] = fresh[c][0:16, 0:128]
                out_ref[3, x] = hx[0:16, 0:128]
                out_ref[4, x] = hy
                out_ref[5, x] = hz

    for n in range(STEPS):
        for first, last, inner in ((n - 4, 0, False), (0, 16, True), (16, 19 - n, False)):

            def step(x, carry, n=n, inner=inner):
                plane_step(n, x, inner)
                return carry

            lax.fori_loop(first, last, step, 0)

    count = count_ref[0, gz]

    def put_tile(t, carry):
        p = place_ref[0, gz, t]
        live = jnp.where(t < count, 1.0, 0.0)
        rows = pl.ds(pl.multiple_of((p & 1) * 8, 8), 8)
        for o in range(8):
            cur_ref[pl.ds(pl.multiple_of(t * 64 + o * 8, 8), 8), :] = phasor_ref[o, p >> 1, rows, :] * live
        return carry

    lax.fori_loop(0, SLOTS, put_tile, 0)


def kernel_options(mib):
    return pltpu.CompilerParams(vmem_limit_bytes=mib << 20)


def shift(block, axis, by):
    count = lax.axis_size(axis)
    pairs = [(i, i + by) for i in range(count) if 0 <= i + by < count]
    return lax.ppermute(block, axis, pairs)


def window(fields, polarization, material, omega0, damping, strength, count, place, index, sizes):
    own = (fields, polarization, material)
    depth = pl.pallas_call(
        pack_depth_kernel,
        out_shape=jax.ShapeDtypeStruct((13, 16, 128), HALO),
        in_specs=[whole()] * 3,
        out_specs=whole(),
        compiler_params=kernel_options(6),
        name="pack_depth",
    )(*own)
    before, after = shift(depth, "gz", 1), shift(depth, "gz", -1)
    low, high = pl.pallas_call(
        pack_x_kernel,
        out_shape=(jax.ShapeDtypeStruct((13, 5, 16, 128), HALO),) * 2,
        in_specs=[whole()] * 5,
        out_specs=(whole(),) * 2,
        compiler_params=kernel_options(6),
        name="pack_x",
    )(*own, before, after)
    left, right = shift(high, "gx", 1), shift(low, "gx", -1)
    low, high = pl.pallas_call(
        pack_y_kernel,
        out_shape=(jax.ShapeDtypeStruct((13, 13, 8, 128), HALO),) * 2,
        in_specs=[whole()] * 7,
        out_specs=(whole(),) * 2,
        compiler_params=kernel_options(6),
        name="pack_y",
    )(*own, before, after, left, right)
    down, up = shift(high, "gy", 1), shift(low, "gy", -1)
    return pl.pallas_call(
        functools.partial(window_kernel, sizes),
        out_shape=(
            jax.ShapeDtypeStruct((6, 16, 16, 128), jnp.float32),
            jax.ShapeDtypeStruct((SLOTS * 64, 128), jnp.float32),
        ),
        in_specs=[scalars()] * 6 + [whole()] * 9,
        out_specs=(whole(),) * 2,
        scratch_shapes=[
            pltpu.VMEM((12, 24, 24, 256), jnp.float32),
            pltpu.VMEM((4, 24, 24, 256), jnp.float32),
            pltpu.VMEM((8, 16, 16, 128), jnp.float32),
        ],
        compiler_params=kernel_options(24),
        name="window",
    )(place, count, index, omega0, damping, strength, *own, before, after, left, right, down, up)


TWO_PI = 2.0 * math.pi
TURN = 0.35 / TWO_PI
PAIRS = 4 * SLOTS


def sin_quarter(y):
    z = y * y
    c = [TWO_PI ** n * s / math.factorial(n) for n, s in ((1, 1), (3, -1), (5, 1), (7, -1), (9, 1), (11, -1))]
    acc = jnp.full_like(z, c[5])
    for k in (4, 3, 2, 1, 0):
        acc = acc * z + c[k]
    return acc * y


def cos_sin(turns):
    r = turns - jnp.floor(turns + 0.5)
    a = jnp.abs(r)
    cos = sin_quarter(0.25 - a)
    sin = sin_quarter(0.25 - jnp.abs(a - 0.25))
    return cos, jnp.where(r < 0, -sin, sin)


def dirs_kernel(angles_ref, order_ref, u_ref):
    idx = order_ref[...]
    hi = idx >> 7
    lo = idx & 127

    def body(h, acc):
        polar, azim = acc
        pick = hi == h
        row_p = jnp.broadcast_to(angles_ref[0, pl.ds(h, 1), :], lo.shape)
        row_a = jnp.broadcast_to(angles_ref[1, pl.ds(h, 1), :], lo.shape)
        polar = jnp.where(pick, jnp.take_along_axis(row_p, lo, axis=1), polar)
        azim = jnp.where(pick, jnp.take_along_axis(row_a, lo, axis=1), azim)
        return polar, azim

    zero = jnp.zeros(idx.shape, jnp.float32)
    polar, azim = lax.fori_loop(0, 64, body, (zero, zero))
    cos_p, sin_p = cos_sin(polar * (1.0 / TWO_PI))
    cos_a, sin_a = cos_sin(azim * (1.0 / TWO_PI))
    u_ref[0] = sin_p * cos_a
    u_ref[1] = sin_p * sin_a
    u_ref[2] = cos_p


def directions(dir_angles, dir_order):
    order = dir_order.reshape(256, 32).T.reshape(64, 128)
    return pl.pallas_call(
        dirs_kernel,
        out_shape=jax.ShapeDtypeStruct((3, 64, 128), jnp.float32),
        in_specs=[pl.BlockSpec(memory_space=pltpu.VMEM)] * 2,
        out_specs=pl.BlockSpec(memory_space=pltpu.VMEM),
        cost_estimate=pl.CostEstimate(flops=3000000, bytes_accessed=300000, transcendentals=0),
        compiler_params=kernel_options(12),
        name="dirs",
    )(dir_angles.reshape(2, 64, 128), order)


def tables_kernel(place_ref, index_ref, u_ref, table_ref, weight_ref, pos_ref):
    @pl.when(pl.program_id(0) == 0)
    def _():
        gx, gy, gz = index_ref[0], index_ref[1], index_ref[2]
        pos_ref[...] = jnp.zeros_like(pos_ref)
        for t in range(SLOTS):
            p = place_ref[0, gz, t]
            for axis, start in enumerate((gx * 16 + (p >> 1), gy * 16 + (p & 1) * 8, gz * 128)):
                pos_ref[axis, t : t + 1, :] = jnp.full((1, 256), start.astype(jnp.float32))

    j2 = pl.multiple_of(pl.program_id(0) * 2, 2)

    def row(axis):
        return jnp.concatenate(
            [u_ref[axis, pl.ds(j2, 1), :], u_ref[axis, pl.ds(j2 + 1, 1), :]], axis=1
        ) * TURN

    ux, uy, uz = row(0), row(1), row(2)
    eight = lax.broadcasted_iota(jnp.int32, (8, 256), 0).astype(jnp.float32)
    sixteen = lax.broadcasted_iota(jnp.int32, (16, 256), 0).astype(jnp.float32) * 8.0
    low_c, low_s = cos_sin(uz * eight)
    high_c, high_s = cos_sin(uz * sixteen)
    row_c, row_s = cos_sin(uy * eight)
    one_c, one_s = row_c[1:2], row_s[1:2]
    for pair in range(8):
        rows = ([], [], [], [])
        for half in range(2):
            a = 2 * pair + half
            hc, hs = high_c[a : a + 1], high_s[a : a + 1]
            c = hc * low_c - hs * low_s
            s = hs * low_c + hc * low_s
            rows[0].append(c)
            rows[1].append(c * one_c - s * one_s)
            rows[2].append(s)
            rows[3].append(s * one_c + c * one_s)
        for part in range(4):
            table_ref[0, part * 128 + 16 * pair : part * 128 + 16 * pair + 16, :] = jnp.concatenate(
                rows[part], axis=0
            ).astype(jnp.bfloat16)
    phase = pos_ref[0] * ux + pos_ref[1] * uy + pos_ref[2] * uz
    tile_c, tile_s = cos_sin(phase)
    for g in range(4):
        gc, gs = row_c[2 * g : 2 * g + 1], row_s[2 * g : 2 * g + 1]
        weight_ref[0, 0, 24 * g : 24 * g + 24, :] = tile_c * gc - tile_s * gs
        weight_ref[0, 1, 24 * g : 24 * g + 24, :] = tile_s * gc + tile_c * gs


def tables(u, place, index):
    return pl.pallas_call(
        tables_kernel,
        grid=(32,),
        out_shape=(
            jax.ShapeDtypeStruct((32, 512, 256), jnp.bfloat16),
            jax.ShapeDtypeStruct((32, 2, 96, 256), jnp.float32),
        ),
        in_specs=[
            scalars(),
            scalars(),
            pl.BlockSpec((3, 64, 128), lambda j: (0, 0, 0)),
        ],
        out_specs=(
            pl.BlockSpec((1, 512, 256), lambda j: (j, 0, 0)),
            pl.BlockSpec((1, 2, 96, 256), lambda j: (j, 0, 0, 0)),
        ),
        scratch_shapes=[pltpu.VMEM((3, 24, 256), jnp.float32)],
        cost_estimate=pl.CostEstimate(flops=60000000, bytes_accessed=14000000, transcendentals=0),
        compiler_params=kernel_options(12),
        name="tables",
    )(place, index, u)


def far_kernel(scale, cur_ref, table_ref, weight_ref, out_ref, lhs_ref, acc_ref):
    j = pl.program_id(0)

    @pl.when(j == 0)
    def _():
        sign = jnp.where(lax.broadcasted_iota(jnp.int32, (SLOTS * 8, 128), 0) % 8 < 4, -1.0, 1.0)
        for ty in range(8):
            g, half = ty // 2, ty % 2
            plain = cur_ref[pl.ds(ty, SLOTS * 8, stride=8), :]
            swapped = pltpu.roll(plain.reshape(SLOTS, 8, 128), 4, 1).reshape(SLOTS * 8, 128) * sign
            rows = slice(g * SLOTS * 8, (g + 1) * SLOTS * 8)
            lhs_ref[rows, half * 128 : half * 128 + 128] = plain.astype(jnp.bfloat16)
            lhs_ref[rows, 256 + half * 128 : 384 + half * 128] = swapped.astype(jnp.bfloat16)

    prod = jnp.dot(lhs_ref[...], table_ref[0], preferred_element_type=jnp.float32)
    first = jnp.zeros((8, 256), jnp.float32)
    second = jnp.zeros((8, 256), jnp.float32)
    for g in range(4):
        for t in range(SLOTS):
            row = 8 * (g * SLOTS + t)
            piece = prod[row : row + 8]
            first = first + piece * weight_ref[0, 0, pl.ds(24 * g + t, 8, stride=0), :]
            second = second + piece * weight_ref[0, 1, pl.ds(24 * g + t, 8, stride=0), :]
    sign = jnp.where(lax.broadcasted_iota(jnp.int32, (8, 256), 0) < 4, -scale, scale)
    acc_ref[pl.ds(pl.multiple_of(j * 8, 8), 8), :] = first * scale + pltpu.roll(second, 4, 0) * sign

    @pl.when(j == pl.num_programs(0) - 1)
    def _():
        out_ref[...] = acc_ref[...].T.astype(out_ref.dtype)


def far_products(currents, table, weight, scale, dtype):
    return pl.pallas_call(
        functools.partial(far_kernel, scale),
        grid=(32,),
        out_shape=jax.ShapeDtypeStruct((256, 256), dtype),
        in_specs=[
            pl.BlockSpec((SLOTS * 64, 128), lambda j: (0, 0)),
            pl.BlockSpec((1, 512, 256), lambda j: (j, 0, 0)),
            pl.BlockSpec((1, 2, 96, 256), lambda j: (j, 0, 0, 0)),
        ],
        out_specs=pl.BlockSpec((256, 256), lambda j: (0, 0)),
        scratch_shapes=[
            pltpu.VMEM((4 * SLOTS * 8, 512), jnp.bfloat16),
            pltpu.VMEM((256, 256), jnp.float32),
        ],
        cost_estimate=pl.CostEstimate(flops=5000000000, bytes_accessed=15000000, transcendentals=0),
        compiler_params=kernel_options(12),
        name="far",
    )(currents, table, weight)


def sum_kernel(in_ref, out_ref):
    total = jnp.sum(in_ref[...].astype(jnp.float32), axis=0, keepdims=True)
    spread = jnp.where(
        lax.broadcasted_iota(jnp.int32, (32, 256), 1) // 8 == lax.broadcasted_iota(jnp.int32, (32, 256), 0),
        jnp.broadcast_to(total, (32, 256)),
        0.0,
    )
    row = lax.broadcasted_iota(jnp.int32, (256, 8), 0) % 8
    col = lax.broadcasted_iota(jnp.int32, (256, 8), 1)
    pick = jnp.where((row % 4) * 2 + row // 4 == col, 1.0, 0.0)
    out_ref[...] = jnp.dot(
        spread, pick, preferred_element_type=jnp.float32, precision=lax.Precision.HIGHEST
    )


def sum_sources(received):
    return pl.pallas_call(
        sum_kernel,
        out_shape=jax.ShapeDtypeStruct((32, 8), jnp.float32),
        in_specs=[pl.BlockSpec(memory_space=pltpu.VMEM)],
        out_specs=pl.BlockSpec(memory_space=pltpu.VMEM),
        compiler_params=kernel_options(12),
        name="sum_sources",
    )(received)


def shards(
    fields,
    polarization,
    material,
    omega0,
    damping,
    strength,
    tile_count,
    tile_place,
    dir_angles,
    dir_order,
):
    sizes = tuple(lax.axis_size(axis) * n for axis, n in zip(AXES, fields.shape[1:]))
    index = jnp.stack([lax.axis_index(axis) for axis in AXES]).astype(jnp.int32)
    table, weight = tables(directions(dir_angles, dir_order), tile_place, index)
    fields_out, currents = window(
        fields,
        polarization,
        material,
        omega0,
        damping,
        strength,
        tile_count,
        tile_place,
        index,
        sizes,
    )
    tile_total = math.prod(lax.axis_size(axis) for axis in AXES) * TILE_MEAN
    scale = 1.0 / math.sqrt(tile_total * TY * fields.shape[3])
    partial = far_products(currents, table, weight, scale, jnp.bfloat16)
    received = lax.all_to_all(partial, AXES, 0, 0, tiled=True)
    return fields_out, sum_sources(received)


def solution(mesh):
    return jax.shard_map(
        shards,
        mesh=mesh,
        in_specs=(
            P(None, *AXES),
            P(None, *AXES),
            P(*AXES),
            P(),
            P(),
            P(),
            P(("gx", "gy"), None),
            P(("gx", "gy"), None, None),
            P(),
            P(),
        ),
        out_specs=(P(None, *AXES), P(AXES, None)),
        check_vma=False,
    )
```

time: 700 us -> 119 us (0.17)
  waiting for transfers between devices: 249 us -> 17.1 us
  other arithmetic: 187 us -> 0.75 us
  local copies, waits for them, and re-layouts: 178 us -> 13.4 us
  Pallas kernels: 0 us -> 43.2 us
  loops' own time: 32.8 us -> 0 us
  blocking collectives: 0 us -> 25.4 us
  between operations: 14.8 us -> 0.82 us
  matrix products: 7.62 us -> 0 us
    unnamed x3 -> x0, waiting for transfers between devices: 218 us -> none
    another operation x43 -> x1, other arithmetic: 131 us -> 0.08 us  [shards(): index = jnp.stack([lax.axis_index(axis) for axis in AXES]).astype(jnp.int32)]
    gather x10 -> x0, local copies, waits for them, and re-layouts: 100 us -> none  [the longest x1 45.5 us: shards(): polar_angle = jnp.take(dir_angles[0], dir_order)]
    pallas_call x0 -> x8, Pallas kernels: none -> 43.2 us  [the longest x1 17 us: window(): pl.pallas_call(functools.partial(window_kernel, sizes), out_shape=(jax.Sh...]
    slice x33 -> x0, local copies, waits for them, and re-layouts: 37.6 us -> none  [the longest x16 14.4 us: far_block(): directions[0][None, :] * tile_x[:, None]]
    another operation x1 -> x0, loops' own time: 32.8 us -> none  [shards(): lax.map(block_far, jnp.arange(DIRS // devices_all * lax.axis_size(('gx_0'...]
    all_to_all x0 -> x1, blocking collectives: none -> 25.4 us  [shards(): received = lax.all_to_all(partial, AXES, 0, 0, tiled=True)]
    mul x68 -> x0, other arithmetic: 19.3 us -> none  [the longest x4 9.44 us: shards(): (electric + SPEED * curl_back(magnetic) - wide_sheet * (pol_new - pol_now...]
  transfers between devices with their start and end apart: 8 -> 6, of which waited for: 6 -> 3; matrix products, arithmetic and copies ran while one was open for 16% -> 2% of each run, Pallas kernels for 0% -> 12%
where the time goes in v1:
time: 119 us; the launch traced here: 118 us
  Pallas kernels  43.2 us (36%)
  blocking collectives  25.4 us (21%)
  starting transfers between devices  17.5 us (15%)
  waiting for transfers between devices  17.1 us (14%)
  local copies, waits for them, and re-layouts  13.4 us (11%)
    all_to_all x1, blocking collectives, shards(): received = lax.all_to_all(partial, AXES, 0, 0, tiled=True)  25.4 us
    ppermute x6, starting transfers between devices, shift(): return lax.ppermute(block, axis, pairs)  17.5 us
    ppermute x6, waiting for transfers between devices, shift(): return lax.ppermute(block, axis, pairs)  17.1 us
    pallas_call x1, Pallas kernels, window(): pl.pallas_call(functools.partial(window_kernel, sizes), out_shape=(jax.Sh...  17 us
    unnamed x29, local copies, waits for them, and re-layouts  11.9 us
    pallas_call x1, Pallas kernels, far_products(): pl.pallas_call(functools.partial(far_kernel, scale), grid=(32,), out_shap...  10.8 us
    pallas_call x1, Pallas kernels, directions(): pl.pallas_call(dirs_kernel, out_shape=jax.ShapeDtypeStruct((3, 64, 128),...  7.16 us
    pallas_call x1, Pallas kernels, tables(): pl.pallas_call(tables_kernel, grid=(32,), out_shape=(jax.ShapeDtypeStruct...  6.73 us
  transfers between devices with their start and end apart: 6, of which 3 were waited for; matrix products, arithmetic and copies ran while one was open for 2% of the time, Pallas kernels for 12%

profile of v1, /device:TPU:1, one launch (start us, length us, event | category | flops | bytes accessed | tf_op | source)
XLA Modules:
  0.0 118.1 jit_solution(14993828229133583121)
XLA Ops:
  0.6 0.0 copy-start
  0.6 1.1 copy-done
  1.8 0.0 copy-start.2
  1.8 1.1 copy-done.2
  2.9 0.0 copy-start.4
  2.9 0.9 copy-done.4
  3.8 0.7 pack_depth.1
  4.5 4.9 %collective-permute-start = (bf16[13,16,128]{2,1,0:T(8,128)(2,1)S(1)}, bf16[13,16,128]{2,1,0:T(8,128)(2,1)S(1)}, u32[]{:S(2)}, u32[]{:S(2)}) collective-permute-start(bf16[13,16,128]{2,1,0:T(8,128)(2,1)S(1)} %pack_depth.1), channel_id=1, source_target_pairs={{0,1},{1,2},{2,3},{4,5},{5,6},{6,7},{8,9},{9,10},{10,11},{12,13},{... | collective-permute-start | bytes 159752 | tf_op jit(solution)/shard_map/ppermute | solution.py:304
  9.5 1.9 %collective-permute-start.1 = (bf16[13,16,128]{2,1,0:T(8,128)(2,1)S(1)}, bf16[13,16,128]{2,1,0:T(8,128)(2,1)S(1)}, u32[]{:S(2)}, u32[]{:S(2)}) collective-permute-start(bf16[13,16,128]{2,1,0:T(8,128)(2,1)S(1)} %pack_depth.1), channel_id=1, source_target_pairs={{1,0},{2,1},{3,2},{5,4},{6,5},{7,6},{9,8},{10,9},{11,10},{13,12},{... | collective-permute-start | bytes 159752 | tf_op jit(solution)/shard_map/ppermute | solution.py:304
  11.4 0.0 collective-permute-done.before_ref
  11.4 3.5 %collective-permute-done.1.after_ref = bf16[13,16,128]{2,1,0:T(8,128)(2,1)S(1)} collective-permute-done((bf16[13,16,128]{2,1,0:T(8,128)(2,1)S(1)}, bf16[13,16,128]{2,1,0:T(8,128)(2,1)S(1)}, u32[]{:S(2)}, u32[]{:S(2)}) %collective-permute-start.1) | collective-permute-done | bytes 53280 | tf_op jit(solution)/shard_map/ppermute | solution.py:304
  14.9 0.1 pack_x.1
  15.0 4.9 %collective-permute-start.2 = (bf16[13,5,16,128]{3,2,1,0:T(8,128)(2,1)S(1)}, bf16[13,5,16,128]{3,2,1,0:T(8,128)(2,1)S(1)}, u32[]{:S(2)}, u32[]{:S(2)}) collective-permute-start(bf16[13,5,16,128]{3,2,1,0:T(8,128)(2,1)S(1)} %get-tuple-element.10), channel_id=1, source_target_pairs={{0,16},{16,32},{32,48},{48,64},{64,80},{80,96},{96,112},{112,128},... | collective-permute-start | bytes 798728 | tf_op jit(solution)/shard_map/ppermute | solution.py:304
  19.9 1.3 %collective-permute-start.3 = (bf16[13,5,16,128]{3,2,1,0:T(8,128)(2,1)S(1)}, bf16[13,5,16,128]{3,2,1,0:T(8,128)(2,1)S(1)}, u32[]{:S(2)}, u32[]{:S(2)}) collective-permute-start(bf16[13,5,16,128]{3,2,1,0:T(8,128)(2,1)S(1)} %get-tuple-element.11), channel_id=1, source_target_pairs={{16,0},{32,16},{48,32},{64,48},{80,64},{96,80},{112,96},{128,112},... | collective-permute-start | bytes 798728 | tf_op jit(solution)/shard_map/ppermute | solution.py:304
  21.2 8.7 %collective-permute-done.2.left_ref = bf16[13,5,16,128]{3,2,1,0:T(8,128)(2,1)S(1)} collective-permute-done((bf16[13,5,16,128]{3,2,1,0:T(8,128)(2,1)S(1)}, bf16[13,5,16,128]{3,2,1,0:T(8,128)(2,1)S(1)}, u32[]{:S(2)}, u32[]{:S(2)}) %collective-permute-start.2) | collective-permute-done | bytes 266272 | tf_op jit(solution)/shard_map/ppermute | solution.py:304
  29.9 4.9 %collective-permute-done.3.right_ref = bf16[13,5,16,128]{3,2,1,0:T(8,128)(2,1)S(1)} collective-permute-done((bf16[13,5,16,128]{3,2,1,0:T(8,128)(2,1)S(1)}, bf16[13,5,16,128]{3,2,1,0:T(8,128)(2,1)S(1)}, u32[]{:S(2)}, u32[]{:S(2)}) %collective-permute-start.3) | collective-permute-done | bytes 266272 | tf_op jit(solution)/shard_map/ppermute | solution.py:304
  34.8 0.5 pack_y.1
  35.3 3.1 %collective-permute-start.4 = (bf16[13,13,8,128]{3,2,1,0:T(8,128)(2,1)S(1)}, bf16[13,13,8,128]{3,2,1,0:T(8,128)(2,1)S(1)}, u32[]{:S(2)}, u32[]{:S(2)}) collective-permute-start(bf16[13,13,8,128]{3,2,1,0:T(8,128)(2,1)S(1)} %get-tuple-element.12), channel_id=1, source_target_pairs={{0,4},{4,8},{8,12},{1,5},{5,9},{9,13},{2,6},{6,10},{10,14},{3,7},{... | collective-permute-start | bytes 1038344 | tf_op jit(solution)/shard_map/ppermute | solution.py:304
  38.5 1.3 %collective-permute-start.5 = (bf16[13,13,8,128]{3,2,1,0:T(8,128)(2,1)S(1)}, bf16[13,13,8,128]{3,2,1,0:T(8,128)(2,1)S(1)}, u32[]{:S(2)}, u32[]{:S(2)}) collective-permute-start(bf16[13,13,8,128]{3,2,1,0:T(8,128)(2,1)S(1)} %get-tuple-element.13), channel_id=1, source_target_pairs={{4,0},{8,4},{12,8},{5,1},{9,5},{13,9},{6,2},{10,6},{14,10},{7,3},{... | collective-permute-start | bytes 1038344 | tf_op jit(solution)/shard_map/ppermute | solution.py:304
  39.8 0.8 copy.26
  40.6 0.8 reshape.16
  41.5 0.1 copy.18
  41.5 7.2 %dirs.1.u_ref = f32[3,64,128]{2,1,0:T(8,128)S(1)} custom-call(f32[2,64,128]{2,1,0:T(8,128)S(1)} %bitcast.13, s32[64,128]{1,0:T(8,128)S(1)} %reshape.17.order_ref), custom_call_target="tpu_custom_call" | custom-call | flops 3000000 | bytes 300000 | tf_op jit(solution)/shard_map/dirs/pallas_call | solution.py:401
  48.7 0.1 pad_add_fusion.index_ref
  48.8 0.0 copy-start.6
  48.8 0.7 copy-done.6
  49.5 6.7 %tables.1 = (bf16[32,512,256]{2,1,0:T(8,128)(2,1)S(1)}, f32[32,2,96,256]{3,2,1,0:T(8,128)S(1)}) custom-call(s32[1,4,18]{2,1,0:T(4,128)S(1)} %copy-done.6, s32[3]{0:T(128)S(1)} %pad_add_fusion.index_ref, f32[3,64,128]{2,1,0:T(8,128)S(1)} %dirs.1.u_ref), custom_call_target="tpu_custom_call" | custom-call | flops 60000000 | bytes 14000000 | tf_op jit(solution)/shard_map/tables/pallas_call | solution.py:460
  56.2 0.0 collective-permute-done.4.down_ref
  56.2 0.0 collective-permute-done.5.up_ref
  56.2 0.0 copy-start.1
  56.2 1.1 copy-done.1
  57.4 0.0 copy-start.3
  57.4 1.1 copy-done.3
  58.5 0.0 copy-start.5
  58.5 0.9 copy-done.5
  59.4 0.0 copy-start.7
  59.4 0.7 copy-done.7
  60.1 0.7 copy-done.8
  60.7 0.7 copy-done.9
  61.4 0.7 copy-done.10
  62.1 0.7 copy-done.11
  62.7 17.0 %window.1 = (f32[6,16,16,128]{3,2,1,0:T(8,128)}, f32[1152,128]{1,0:T(8,128)S(1)}) custom-call(s32[1,4,18]{2,1,0:T(4,128)S(1)} %copy-done.7, s32[1,4]{1,0:T(1,128)S(1)} %copy-done.8, s32[3]{0:T(128)S(1)} %pad_add_fusion.index_ref, f32[4]{0:T(128)S(1)} %copy-done.9, f32[4]{0:T(128)S(1)} %copy-done.10, f32[4]{0:T(128)S(1)} %copy-done.11, ...), custom_call_target="tpu_custom_call" | custom-call | tf_op jit(solution)/shard_map/window/pallas_call | solution.py:336
  79.7 10.8 %far.1 = bf16[256,256]{1,0:T(8,128)(2,1)S(1)} custom-call(f32[1152,128]{1,0:T(8,128)S(1)} %get-tuple-element.15.cur_ref, bf16[32,512,256]{2,1,0:T(8,128)(2,1)S(1)} %get-tuple-element.16.table_ref, f32[32,2,96,256]{3,2,1,0:T(8,128)S(1)} %get-tuple-element.17.weight_ref), custom_call_target="tpu_custom_call" | custom-call | flops 5000000000 | bytes 15000000 | tf_op jit(solution)/shard_map/far/pallas_call | solution.py:515
  90.5 0.5 broadcast
  91.0 0.7 reduce
  91.8 25.4 %all_to_all.11 = bf16[256,2,128]{2,1,0:T(2,128)(2,1)S(1)} all-to-all(bf16[256,2,128]{2,1,0:T(2,128)(2,1)S(1)} %reshape.18), channel_id=1, replica_groups=mesh['gx'=16,'gy'=4,'gz'=4] {'gx','gy','gz'}, dimensions={0} | all-to-all | bytes 262144 | tf_op jit(solution)/shard_map/all_to_all | solution.py:591
  117.2 0.3 sum_sources.1
  117.5 0.7 copy.20
  (8 shorter events, 0.1 us)
Async XLA Ops:
  0.6 1.1 copy-start
  1.8 1.1 copy-start.2
  2.9 0.9 copy-start.4
  4.5 6.9 %collective-permute-start = (bf16[13,16,128]{2,1,0:T(8,128)(2,1)S(1)}, bf16[13,16,128]{2,1,0:T(8,128)(2,1)S(1)}, u32[]{:S(2)}, u32[]{:S(2)}) collective-permute-start(bf16[13,16,128]{2,1,0:T(8,128)(2,1)S(1)} %pack_depth.1), channel_id=1, source_target_pairs={{0,1},{1,2},{2,3},{4,5},{5,6},{6,7},{8,9},{9,10},{10,11},{12,13},{... | collective-permute-start | bytes 159752 | tf_op jit(solution)/shard_map/ppermute | solution.py:304
  9.5 5.5 %collective-permute-start.1 = (bf16[13,16,128]{2,1,0:T(8,128)(2,1)S(1)}, bf16[13,16,128]{2,1,0:T(8,128)(2,1)S(1)}, u32[]{:S(2)}, u32[]{:S(2)}) collective-permute-start(bf16[13,16,128]{2,1,0:T(8,128)(2,1)S(1)} %pack_depth.1), channel_id=1, source_target_pairs={{1,0},{2,1},{3,2},{5,4},{6,5},{7,6},{9,8},{10,9},{11,10},{13,12},{... | collective-permute-start | bytes 159752 | tf_op jit(solution)/shard_map/ppermute | solution.py:304
  15.0 14.9 %collective-permute-start.2 = (bf16[13,5,16,128]{3,2,1,0:T(8,128)(2,1)S(1)}, bf16[13,5,16,128]{3,2,1,0:T(8,128)(2,1)S(1)}, u32[]{:S(2)}, u32[]{:S(2)}) collective-permute-start(bf16[13,5,16,128]{3,2,1,0:T(8,128)(2,1)S(1)} %get-tuple-element.10), channel_id=1, source_target_pairs={{0,16},{16,32},{32,48},{48,64},{64,80},{80,96},{96,112},{112,128},... | collective-permute-start | bytes 798728 | tf_op jit(solution)/shard_map/ppermute | solution.py:304
  19.9 14.9 %collective-permute-start.3 = (bf16[13,5,16,128]{3,2,1,0:T(8,128)(2,1)S(1)}, bf16[13,5,16,128]{3,2,1,0:T(8,128)(2,1)S(1)}, u32[]{:S(2)}, u32[]{:S(2)}) collective-permute-start(bf16[13,5,16,128]{3,2,1,0:T(8,128)(2,1)S(1)} %get-tuple-element.11), channel_id=1, source_target_pairs={{16,0},{32,16},{48,32},{64,48},{80,64},{96,80},{112,96},{128,112},... | collective-permute-start | bytes 798728 | tf_op jit(solution)/shard_map/ppermute | solution.py:304
  35.3 20.9 %collective-permute-start.4 = (bf16[13,13,8,128]{3,2,1,0:T(8,128)(2,1)S(1)}, bf16[13,13,8,128]{3,2,1,0:T(8,128)(2,1)S(1)}, u32[]{:S(2)}, u32[]{:S(2)}) collective-permute-start(bf16[13,13,8,128]{3,2,1,0:T(8,128)(2,1)S(1)} %get-tuple-element.12), channel_id=1, source_target_pairs={{0,4},{4,8},{8,12},{1,5},{5,9},{9,13},{2,6},{6,10},{10,14},{3,7},{... | collective-permute-start | bytes 1038344 | tf_op jit(solution)/shard_map/ppermute | solution.py:304
  38.5 17.8 %collective-permute-start.5 = (bf16[13,13,8,128]{3,2,1,0:T(8,128)(2,1)S(1)}, bf16[13,13,8,128]{3,2,1,0:T(8,128)(2,1)S(1)}, u32[]{:S(2)}, u32[]{:S(2)}) collective-permute-start(bf16[13,13,8,128]{3,2,1,0:T(8,128)(2,1)S(1)} %get-tuple-element.13), channel_id=1, source_target_pairs={{4,0},{8,4},{12,8},{5,1},{9,5},{13,9},{6,2},{10,6},{14,10},{7,3},{... | collective-permute-start | bytes 1038344 | tf_op jit(solution)/shard_map/ppermute | solution.py:304
  48.8 0.7 copy-start.6
  56.2 1.1 copy-start.1
  57.4 1.1 copy-start.3
  58.5 0.9 copy-start.5
  59.4 0.7 copy-start.7
  60.1 0.7 copy-start.8
  60.7 0.7 copy-start.9
  61.4 0.7 copy-start.10
  62.1 0.7 copy-start.11

commit v2 on v1

v2 whole, which is shorter than its diff:
```python
import functools
import math

import jax
import jax.numpy as jnp
from jax import lax
from jax.experimental import pallas as pl
from jax.experimental.pallas import tpu as pltpu
from jax.sharding import PartitionSpec as P

TY = 8
STEPS = 4
TILE_MEAN = 6
SLOTS = 18
SPEED = 0.5
WAVE = 0.35
HALO = jnp.bfloat16
BLOCK = 8
PER_STEP = 4
AXES = ("gx", "gy", "gz")


def whole():
    return pl.BlockSpec(memory_space=pltpu.VMEM)


def scalars():
    return pl.BlockSpec(memory_space=pltpu.SMEM)


def pack_depth_kernel(fields_ref, pol_ref, mat_ref, out_ref, buf_ref, raw_ref, sems):
    lane = lax.broadcasted_iota(jnp.int32, (16, 128), 1) // 8
    copies = [pltpu.make_async_copy(fields_ref.at[a], buf_ref.at[a], sems.at[a]) for a in range(6)]
    copies += [
        pltpu.make_async_copy(pol_ref.at[a], buf_ref.at[a + 6], sems.at[a + 6]) for a in range(6)
    ]
    copies.append(pltpu.make_async_copy(mat_ref, raw_ref, sems.at[12]))
    for copy in copies:
        copy.start()
    for a, copy in enumerate(copies):
        copy.wait()
        acc = jnp.zeros((16, 128), jnp.float32)
        for x in range(16):
            plane = raw_ref[x].astype(jnp.float32) if a == 12 else buf_ref[a, x]
            acc = jnp.where(lane == x, pltpu.roll(plane, (8 * x + 4) % 128, 1), acc)
        out_ref[a] = acc.astype(HALO)


def stage_kernel(fields_ref, pol_ref, mat_ref, own_ref):
    own_ref[0:6] = fields_ref[...]
    own_ref[6:12] = pol_ref[...]
    own_ref[12] = mat_ref[...].astype(jnp.float32)


def join_depth(before, after):
    lane = lax.broadcasted_iota(jnp.int32, (16, 128), 1) % 8
    return jnp.where(lane < 4, before.astype(jnp.float32), after.astype(jnp.float32))


def pack_x_kernel(own_ref, before_ref, after_ref, low_ref, high_ref):
    def body(a, carry):
        for k in range(3):
            low_ref[a * 3 + k] = own_ref[a, k].astype(HALO)
            high_ref[a * 3 + k] = own_ref[a, 13 + k].astype(HALO)
        return carry

    lax.fori_loop(0, 13, body, 0)
    for k, a in enumerate((1, 2)):
        low_ref[39 + k] = own_ref[a, 3].astype(HALO)
    for k, a in enumerate((0, 1, 2, 4, 5)):
        high_ref[39 + k] = own_ref[a, 12].astype(HALO)
    group = lax.broadcasted_iota(jnp.int32, (16, 128), 1) // 32
    for q in range(4):
        low = jnp.zeros((16, 128), jnp.float32)
        high = low
        for r in range(min(4, 13 - 4 * q)):
            depth = join_depth(before_ref[4 * q + r], after_ref[4 * q + r])
            low = jnp.where(group == r, pltpu.roll(depth, 32 * r, 1) if r else depth, low)
            high = jnp.where(group == r, pltpu.roll(depth, 32 * r + 32, 1) if r < 3 else depth, high)
        low_ref[41 + q] = low.astype(HALO)
        high_ref[44 + q] = high.astype(HALO)


def wide_plane(x, a, own_ref, before_ref, after_ref, left_ref, right_ref):
    if x < 16:
        return own_ref[a, x]
    if x < 19:
        return right_ref[a * 3 + x - 16].astype(jnp.float32)
    if x == 19:
        return right_ref[39 + jnp.clip(a - 1, 0, 1)].astype(jnp.float32)
    if x == 20:
        return left_ref[39 + jnp.minimum(jnp.where(a < 3, a, a - 1), 4)].astype(jnp.float32)
    if x < 24:
        return left_ref[a * 3 + x - 21].astype(jnp.float32)
    if x == 24:
        return join_depth(before_ref[a], after_ref[a])
    lane = lax.broadcasted_iota(jnp.int32, (16, 128), 1)
    turn = 32 * (a % 4)
    return jnp.where(
        lane < 32,
        pltpu.roll(right_ref[41 + a // 4].astype(jnp.float32), (128 - turn) % 128, 1),
        pltpu.roll(left_ref[44 + a // 4].astype(jnp.float32), (160 - turn) % 128, 1),
    )


def pack_y_kernel(
    own_ref, before_ref, after_ref, left_ref, right_ref, u_ref, low_ref, high_ref
):
    top = lax.broadcasted_iota(jnp.int32, (8, 128), 0) < 4

    def body(a, carry):
        for i in range(13):
            p0, p1 = [
                wide_plane(2 * i + k, a, own_ref, before_ref, after_ref, left_ref, right_ref)
                for k in range(2)
            ]
            low_ref[a, i] = jnp.where(top, p0[0:8], pltpu.roll(p1[0:8], 4, 0)).astype(HALO)
            high_ref[a, i] = jnp.where(top, pltpu.roll(p1[8:16], 4, 0), p0[8:16]).astype(HALO)
        return carry

    lax.fori_loop(0, 13, body, 0)


def side_lanes(depth, x):
    return pltpu.roll(depth[x // 16], (124 - 8 * x) % 128, 1)


def coefficients(medium_ref, value):
    shape = value.shape
    a = jnp.zeros(shape, jnp.float32)
    b, c = a, a
    for m in range(4):
        omega = jnp.full((8, 128), medium_ref[m], jnp.float32)
        half = 0.5 * jnp.full((8, 128), medium_ref[4 + m], jnp.float32)
        strong = jnp.full((8, 128), medium_ref[8 + m], jnp.float32)
        square = omega * omega
        under = 1.0 + half
        hit = value == float(m + 1)
        wide = (lambda v: jnp.broadcast_to(jnp.concatenate([v[0:1]] * 2, axis=1), shape))
        a = jnp.where(hit, wide((2.0 - square) / under), a)
        b = jnp.where(hit, wide(-(1.0 - half) / under), b)
        c = jnp.where(hit, wide(strong * square / under), c)
    return a, b, c, jnp.where(value > 0.0, 1.0, 0.0)


def lay_kernel(
    medium_ref, own_ref, before_ref, after_ref, left_ref, right_ref, low_ref, wide_ref, coef_ref
):
    def spread(a, store):
        depth = [
            wide_plane(24 + k, a, own_ref, before_ref, after_ref, left_ref, right_ref)
            for k in range(2)
        ]
        for x in range(24):
            main = wide_plane(x, a, own_ref, before_ref, after_ref, left_ref, right_ref)
            store(x, jnp.concatenate([main, side_lanes(depth, x)], axis=1))

    def body(a, carry):
        def store(x, value):
            wide_ref[a, x] = value

        spread(a, store)
        return carry

    lax.fori_loop(0, 12, body, 0)

    def store_coef(x, value):
        for k, coef in enumerate(coefficients(medium_ref, value)):
            coef_ref[k, x] = coef

    spread(jnp.int32(12), store_coef)


def window_kernel(
    extents,
    ints_ref,
    medium_ref,
    laid_ref,
    laid_coef_ref,
    down_ref,
    up_ref,
    out_ref,
    cur_ref,
    wide_ref,
    tail_ref,
    tail_coef_ref,
    phasor_ref,
):
    top = lax.broadcasted_iota(jnp.int32, (8, 128), 0) < 4

    def spread(a, store):
        def rows(i):
            lowest = up_ref[a, i].astype(jnp.float32)
            highest = down_ref[a, i].astype(jnp.float32)
            return (
                jnp.where(top, lowest, highest),
                pltpu.roll(jnp.where(top, highest, lowest), 4, 0),
            )

        depth = rows(12)
        for i in range(12):
            tail = rows(i)
            for k in range(2):
                x = 2 * i + k
                store(x, jnp.concatenate([tail[k], side_lanes(depth, x)], axis=1))

    def body(a, carry):
        def store(x, value):
            tail_ref[a, x] = value

        spread(a, store)
        return carry

    lax.fori_loop(0, 12, body, 0)

    def store_coef(x, value):
        for k, coef in enumerate(coefficients(medium_ref, value)):
            tail_coef_ref[k, x] = coef

    spread(12, store_coef)

    def first_value(k, x):
        return jnp.concatenate([laid_ref[k, x], tail_ref[k, x]], axis=0)

    def coefficient(k, x):
        return jnp.concatenate([laid_coef_ref[k, x], tail_coef_ref[k, x]], axis=0)

    gx, gy, gz = ints_ref[76], ints_ref[77], ints_ref[78]
    row = lax.broadcasted_iota(jnp.int32, (24, 256), 0)
    row = jnp.where(row < 20, row, row - 24) + gy * 16
    lane = lax.broadcasted_iota(jnp.int32, (24, 256), 1)
    near = (lane < 132) | (lane >= 252)
    lane = jnp.where(lane < 132, lane, lane - 256) + gz * 128
    inside = near & (row >= 0) & (row < extents[1]) & (lane >= 0) & (lane < extents[2])
    inside = jnp.where(inside, SPEED, 0.0).astype(jnp.float32)

    def ahead_y(v):
        return pltpu.roll(v, 23, 0)

    def behind_y(v):
        return pltpu.roll(v, 1, 0)

    def ahead_z(v):
        return pltpu.roll(v, 255, 1)

    def behind_z(v):
        return pltpu.roll(v, 1, 1)

    def wrap(x):
        return jnp.where(x < 0, x + 24, x) if not isinstance(x, int) else x % 24

    def magnetic_step(n, x):
        here, after = wrap(x), wrap(x + 1)
        place = gx * 16 + x
        speed = inside * jnp.where((place >= 0) & (place < extents[0]), 1.0, 0.0)
        get = first_value if n == 0 else (lambda k, at: wide_ref[k, at])
        ex, ey, ez = get(0, here), get(1, here), get(2, here)
        ey_next, ez_next = get(1, after), get(2, after)
        hx = get(3, here) - speed * ((ahead_y(ez) - ez) - (ahead_z(ey) - ey))
        hy = get(4, here) - speed * ((ahead_z(ex) - ex) - (ez_next - ez))
        hz = get(5, here) - speed * ((ey_next - ey) - (ahead_y(ex) - ex))
        wide_ref[3, here] = hx
        wide_ref[4, here] = hy
        wide_ref[5, here] = hz
        return speed, hx, hy, hz

    def electric_step(n, x, inner, speed, hx, hy, hz):
        here, prior = wrap(x), wrap(x - 1)
        last = n == STEPS - 1

        def cut(v):
            return v[0:16, 0:128] if last else v

        now, old = (6, 9) if n % 2 == 0 else (9, 6)

        def get(k, at, fresh=True):
            if fresh and (n == 0 or (n == 1 and k >= 6 and k < 9)):
                return first_value(k, at)
            return wide_ref[k, at, 0:16, 0:128] if last else wide_ref[k, at]

        def get_coef(k):
            return laid_coef_ref[k, here, 0:16, 0:128] if last else coefficient(k, here)

        def put(k, value):
            if last:
                wide_ref[k, here, 0:16, 0:128] = value
            else:
                wide_ref[k, here] = value

        ex, ey, ez = get(0, here), get(1, here), get(2, here)
        hy_prior, hz_prior = get(4, prior, False), get(5, prior, False)
        sat = 1.0 / (1.0 + ex * ex + ey * ey + ez * ez)
        a, b, sheet = get_coef(0), get_coef(1), get_coef(3)
        drive = get_coef(2) * sat
        hxc, hyc, hzc = cut(hx), cut(hy), cut(hz)
        curls = (
            (hzc - cut(behind_y(hz))) - (hyc - cut(behind_z(hy))),
            (hxc - cut(behind_z(hx))) - (hzc - hz_prior),
            (hyc - hy_prior) - (hxc - cut(behind_y(hx))),
        )
        rate = cut(speed)
        fresh = []
        for c, e in enumerate((ex, ey, ez)):
            pol = get(now + c, here)
            pol_new = a * pol + b * get(old + c, here) + drive * e
            value = e + rate * curls[c] - sheet * (pol_new - pol)
            if last:
                out_ref[c, x] = value
            else:
                put(old + c, pol_new)
                put(c, value)
            fresh.append(value)
        if inner:
            angle_h = WAVE * SPEED * (n + 0.5)
            angle_e = WAVE * SPEED * (n + 1.0)
            hxc, hyc, hzc = hx[0:16, 0:128], hy[0:16, 0:128], hz[0:16, 0:128]
            ey, ez = fresh[1][0:16, 0:128], fresh[2][0:16, 0:128]
            terms = (
                (-math.cos(angle_h), hzc),
                (math.cos(angle_h), hyc),
                (math.cos(angle_e), ez),
                (-math.cos(angle_e), ey),
                (math.sin(angle_h), hzc),
                (-math.sin(angle_h), hyc),
                (-math.sin(angle_e), ez),
                (math.sin(angle_e), ey),
            )
            for o, (factor, value) in enumerate(terms):
                phasor_ref[o, x] = factor * value if n == 0 else phasor_ref[o, x] + factor * value
            if last:
                out_ref[3, x] = hxc
                out_ref[4, x] = hyc
                out_ref[5, x] = hzc

    def block_step(n, first, count, inner):
        states = [magnetic_step(n, first + k) for k in range(count)]
        if n == STEPS - 1 and not inner:
            return
        for k, state in enumerate(states):
            electric_step(n, first + k, inner, *state)

    for k in (4, 5):
        wide_ref[k, 19] = jnp.zeros((24, 256), jnp.float32)

    for n in range(STEPS):
        block_step(n, n - 4, 4 - n, False)

        def step(i, carry, n=n):
            block_step(n, i * BLOCK, BLOCK, True)
            return carry

        lax.fori_loop(0, 16 // BLOCK, step, 0)
        if n < STEPS - 1:
            block_step(n, 16, 3 - n, False)

    count = ints_ref[72 + gz]

    def put_tile(t, carry):
        p = ints_ref[gz * SLOTS + t]
        live = jnp.where(t < count, 1.0, 0.0)
        rows = pl.ds(pl.multiple_of((p & 1) * 8, 8), 8)
        for o in range(8):
            cur_ref[pl.ds(pl.multiple_of(t * 64 + o * 8, 8), 8), :] = phasor_ref[o, p >> 1, rows, :] * live
        return carry

    lax.fori_loop(0, SLOTS, put_tile, 0)


def kernel_options(mib):
    return pltpu.CompilerParams(vmem_limit_bytes=mib << 20)


def shift(block, axis, by):
    count = lax.axis_size(axis)
    pairs = [(i, i + by) for i in range(count) if 0 <= i + by < count]
    return lax.ppermute(block, axis, pairs)


def window(fields, polarization, material, medium, ints, sizes, dir_angles, dir_order):
    anywhere = pl.BlockSpec(memory_space=pl.ANY)
    depth = pl.pallas_call(
        pack_depth_kernel,
        out_shape=jax.ShapeDtypeStruct((13, 16, 128), HALO),
        in_specs=[pl.BlockSpec(memory_space=pltpu.HBM)] * 3,
        out_specs=whole(),
        scratch_shapes=[
            pltpu.VMEM((12, 16, 16, 128), jnp.float32),
            pltpu.VMEM((16, 16, 128), jnp.int32),
            pltpu.SemaphoreType.DMA((13,)),
        ],
        compiler_params=pltpu.CompilerParams(vmem_limit_bytes=65000 << 10),
        name="pack_depth",
    )(fields, polarization, material)
    later, _ = lax.optimization_barrier(((fields, polarization, material), depth))
    own = pl.pallas_call(
        stage_kernel,
        out_shape=jax.ShapeDtypeStruct((13, 16, 16, 128), jnp.float32),
        in_specs=[whole()] * 3,
        out_specs=whole(),
        compiler_params=kernel_options(6),
        name="stage",
    )(*later)
    before, after = shift(depth, "gz", 1), shift(depth, "gz", -1)
    low, high = pl.pallas_call(
        pack_x_kernel,
        out_shape=(
            jax.ShapeDtypeStruct((45, 16, 128), HALO),
            jax.ShapeDtypeStruct((48, 16, 128), HALO),
        ),
        in_specs=[whole()] * 3,
        out_specs=(whole(),) * 2,
        compiler_params=kernel_options(6),
        name="pack_x",
    )(own, before, after)
    left, right = shift(high, "gx", 1), shift(low, "gx", -1)
    u = directions(dir_angles, dir_order, low)
    table, weight = tables(u, ints, low)
    low, high = pl.pallas_call(
        pack_y_kernel,
        out_shape=(jax.ShapeDtypeStruct((13, 13, 8, 128), HALO),) * 2,
        in_specs=[whole()] * 5 + [anywhere],
        out_specs=(whole(),) * 2,
        compiler_params=kernel_options(6),
        name="pack_y",
    )(own, before, after, left, right, weight)
    laid, laid_coef = pl.pallas_call(
        lay_kernel,
        out_shape=(
            jax.ShapeDtypeStruct((12, 24, 16, 256), jnp.float32),
            jax.ShapeDtypeStruct((4, 24, 16, 256), jnp.float32),
        ),
        in_specs=[scalars()] + [whole()] * 5 + [anywhere],
        out_specs=(whole(),) * 2,
        compiler_params=kernel_options(10),
        cost_estimate=pl.CostEstimate(flops=8000000, bytes_accessed=9000000, transcendentals=0),
        name="lay",
    )(medium, own, before, after, left, right, low)
    down, up = shift(high, "gy", 1), shift(low, "gy", -1)
    fields_out, currents = pl.pallas_call(
        functools.partial(window_kernel, sizes),
        out_shape=(
            jax.ShapeDtypeStruct((6, 16, 16, 128), jnp.float32),
            jax.ShapeDtypeStruct((SLOTS * 64, 128), jnp.float32),
        ),
        in_specs=[scalars()] * 2 + [whole()] * 4,
        out_specs=(whole(),) * 2,
        scratch_shapes=[
            pltpu.VMEM((12, 24, 24, 256), jnp.float32),
            pltpu.VMEM((12, 24, 8, 256), jnp.float32),
            pltpu.VMEM((4, 24, 8, 256), jnp.float32),
            pltpu.VMEM((8, 16, 16, 128), jnp.float32),
        ],
        compiler_params=kernel_options(24),
        name="window",
    )(ints, medium, laid, laid_coef, down, up)
    return fields_out, currents, table, weight


TWO_PI = 2.0 * math.pi
TURN = 0.35 / TWO_PI
PAIRS = 4 * SLOTS


def sin_quarter(y):
    z = y * y
    c = [TWO_PI ** n * s / math.factorial(n) for n, s in ((1, 1), (3, -1), (5, 1), (7, -1), (9, 1), (11, -1))]
    acc = jnp.full_like(z, c[5])
    for k in (4, 3, 2, 1, 0):
        acc = acc * z + c[k]
    return acc * y


def cos_sin(turns):
    r = turns - jnp.floor(turns + 0.5)
    a = jnp.abs(r)
    cos = sin_quarter(0.25 - a)
    sin = sin_quarter(0.25 - jnp.abs(a - 0.25))
    return cos, jnp.where(r < 0, -sin, sin)


def dirs_kernel(angles_ref, order_ref, low_ref, u_ref):
    idx = order_ref[...]
    hi = idx >> 7
    lo = idx & 127

    def body(h, acc):
        polar, azim = acc
        pick = hi == h
        row_p = jnp.broadcast_to(angles_ref[0, pl.ds(h, 1), :], lo.shape)
        row_a = jnp.broadcast_to(angles_ref[1, pl.ds(h, 1), :], lo.shape)
        polar = jnp.where(pick, jnp.take_along_axis(row_p, lo, axis=1), polar)
        azim = jnp.where(pick, jnp.take_along_axis(row_a, lo, axis=1), azim)
        return polar, azim

    zero = jnp.zeros(idx.shape, jnp.float32)
    polar, azim = lax.fori_loop(0, 64, body, (zero, zero), unroll=4)
    cos_p, sin_p = cos_sin(polar * (1.0 / TWO_PI))
    cos_a, sin_a = cos_sin(azim * (1.0 / TWO_PI))
    u_ref[0] = sin_p * cos_a
    u_ref[1] = sin_p * sin_a
    u_ref[2] = cos_p


def directions(dir_angles, dir_order, low):
    order = dir_order.reshape(256, 32).T.reshape(64, 128)
    return pl.pallas_call(
        dirs_kernel,
        out_shape=jax.ShapeDtypeStruct((3, 64, 128), jnp.float32),
        in_specs=[whole(), whole(), pl.BlockSpec(memory_space=pl.ANY)],
        out_specs=whole(),
        cost_estimate=pl.CostEstimate(flops=3000000, bytes_accessed=300000, transcendentals=0),
        compiler_params=kernel_options(12),
        name="dirs",
    )(dir_angles.reshape(2, 64, 128), order, low)


def tables_kernel(ints_ref, low_ref, u_ref, table_ref, weight_ref, pos_ref):
    @pl.when(pl.program_id(0) == 0)
    def _():
        gx, gy, gz = ints_ref[76], ints_ref[77], ints_ref[78]
        pos_ref[...] = jnp.zeros_like(pos_ref)
        for t in range(SLOTS):
            p = ints_ref[gz * SLOTS + t]
            for axis, start in enumerate((gx * 16 + (p >> 1), gy * 16 + (p & 1) * 8, gz * 128)):
                pos_ref[axis, t : t + 1, :] = jnp.full((1, 256), start.astype(jnp.float32))

    j2 = pl.multiple_of(pl.program_id(0) * 2, 2)

    def row(axis):
        return jnp.concatenate(
            [u_ref[axis, pl.ds(j2, 1), :], u_ref[axis, pl.ds(j2 + 1, 1), :]], axis=1
        ) * TURN

    ux, uy, uz = row(0), row(1), row(2)
    eight = lax.broadcasted_iota(jnp.int32, (8, 256), 0).astype(jnp.float32)
    sixteen = lax.broadcasted_iota(jnp.int32, (16, 256), 0).astype(jnp.float32) * 8.0
    low_c, low_s = cos_sin(uz * eight)
    high_c, high_s = cos_sin(uz * sixteen)
    row_c, row_s = cos_sin(uy * eight)
    one_c, one_s = row_c[1:2], row_s[1:2]
    for pair in range(8):
        rows = ([], [], [], [])
        for half in range(2):
            a = 2 * pair + half
            hc, hs = high_c[a : a + 1], high_s[a : a + 1]
            c = hc * low_c - hs * low_s
            s = hs * low_c + hc * low_s
            rows[0].append(c)
            rows[1].append(c * one_c - s * one_s)
            rows[2].append(s)
            rows[3].append(s * one_c + c * one_s)
        for part in range(4):
            table_ref[0, part * 128 + 16 * pair : part * 128 + 16 * pair + 16, :] = jnp.concatenate(
                rows[part], axis=0
            ).astype(jnp.bfloat16)
    phase = pos_ref[0] * ux + pos_ref[1] * uy + pos_ref[2] * uz
    tile_c, tile_s = cos_sin(phase)
    for g in range(4):
        gc, gs = row_c[2 * g : 2 * g + 1], row_s[2 * g : 2 * g + 1]
        weight_ref[0, 0, 24 * g : 24 * g + 24, :] = tile_c * gc - tile_s * gs
        weight_ref[0, 1, 24 * g : 24 * g + 24, :] = tile_s * gc + tile_c * gs


def tables(u, ints, low):
    return pl.pallas_call(
        tables_kernel,
        grid=(32,),
        out_shape=(
            jax.ShapeDtypeStruct((32, 512, 256), jnp.bfloat16),
            jax.ShapeDtypeStruct((32, 2, 96, 256), jnp.float32),
        ),
        in_specs=[
            scalars(),
            pl.BlockSpec(memory_space=pl.ANY),
            pl.BlockSpec((3, 64, 128), lambda j: (0, 0, 0)),
        ],
        out_specs=(
            pl.BlockSpec((1, 512, 256), lambda j: (j, 0, 0)),
            pl.BlockSpec((1, 2, 96, 256), lambda j: (j, 0, 0, 0)),
        ),
        scratch_shapes=[pltpu.VMEM((3, 24, 256), jnp.float32)],
        cost_estimate=pl.CostEstimate(flops=60000000, bytes_accessed=14000000, transcendentals=0),
        compiler_params=kernel_options(12),
        name="tables",
    )(ints, low, u)


def far_kernel(scale, cur_ref, table_ref, weight_ref, out_ref, lhs_ref, acc_ref, rows_ref):
    j = pl.program_id(0)

    @pl.when(j == 0)
    def _():
        sign = jnp.where(lax.broadcasted_iota(jnp.int32, (SLOTS * 8, 128), 0) % 8 < 4, -1.0, 1.0)
        for ty in range(8):
            g, half = ty // 2, ty % 2
            plain = cur_ref[pl.ds(ty, SLOTS * 8, stride=8), :]
            swapped = pltpu.roll(plain.reshape(SLOTS, 8, 128), 4, 1).reshape(SLOTS * 8, 128) * sign
            rows = slice(g * SLOTS * 8, (g + 1) * SLOTS * 8)
            lhs_ref[rows, half * 128 : half * 128 + 128] = plain.astype(jnp.bfloat16)
            lhs_ref[rows, 256 + half * 128 : 384 + half * 128] = swapped.astype(jnp.bfloat16)

    for k in range(PER_STEP):
        far_block(scale, j * PER_STEP + k, k, lhs_ref, table_ref, weight_ref, acc_ref)

    @pl.when(j == pl.num_programs(0) - 1)
    def _():
        turned = acc_ref[...].T
        rows_ref[pl.ds(0, 256, stride=2), :] = turned[:, 0:128]
        rows_ref[pl.ds(1, 256, stride=2), :] = turned[:, 128:256]
        out_ref[...] = rows_ref[...].astype(out_ref.dtype)


def far_block(scale, j, k, lhs_ref, table_ref, weight_ref, acc_ref):
    prod = jnp.dot(lhs_ref[...], table_ref[k], preferred_element_type=jnp.float32)
    first = jnp.zeros((8, 256), jnp.float32)
    second = jnp.zeros((8, 256), jnp.float32)
    for g in range(4):
        for t in range(SLOTS):
            row = 8 * (g * SLOTS + t)
            piece = prod[row : row + 8]
            first = first + piece * weight_ref[k, 0, pl.ds(24 * g + t, 8, stride=0), :]
            second = second + piece * weight_ref[k, 1, pl.ds(24 * g + t, 8, stride=0), :]
    sign = jnp.where(lax.broadcasted_iota(jnp.int32, (8, 256), 0) < 4, -scale, scale)
    acc_ref[pl.ds(pl.multiple_of(j * 8, 8), 8), :] = first * scale + pltpu.roll(second, 4, 0) * sign


def far_products(currents, table, weight, scale, dtype):
    return pl.pallas_call(
        functools.partial(far_kernel, scale),
        grid=(32 // PER_STEP,),
        out_shape=jax.ShapeDtypeStruct((512, 128), dtype),
        in_specs=[
            pl.BlockSpec((SLOTS * 64, 128), lambda j: (0, 0)),
            pl.BlockSpec((PER_STEP, 512, 256), lambda j: (j, 0, 0)),
            pl.BlockSpec((PER_STEP, 2, 96, 256), lambda j: (j, 0, 0, 0)),
        ],
        out_specs=pl.BlockSpec((512, 128), lambda j: (0, 0)),
        scratch_shapes=[
            pltpu.VMEM((4 * SLOTS * 8, 512), jnp.bfloat16),
            pltpu.VMEM((256, 256), jnp.float32),
            pltpu.VMEM((512, 128), jnp.float32),
        ],
        cost_estimate=pl.CostEstimate(flops=5000000000, bytes_accessed=15000000, transcendentals=0),
        compiler_params=kernel_options(12),
        name="far",
    )(currents, table, weight)


def sum_kernel(in_ref, out_ref):
    eight = jnp.sum(in_ref[...].astype(jnp.float32).reshape(64, 8, 128), axis=0)
    halves = [sum(eight[k : k + 1] for k in range(h + 2, 8, 2)) + eight[h : h + 1] for h in range(2)]
    total = jnp.concatenate(halves, axis=1)
    row = lax.broadcasted_iota(jnp.int32, (8, 256), 0)
    col = lax.broadcasted_iota(jnp.int32, (8, 256), 1) % 8
    spread = jnp.where((row % 2) * 4 + row // 2 == col, jnp.broadcast_to(total, (8, 256)), 0.0)
    pick = jnp.where(
        lax.broadcasted_iota(jnp.int32, (256, 32), 0) // 8
        == lax.broadcasted_iota(jnp.int32, (256, 32), 1),
        1.0,
        0.0,
    )
    out_ref[...] = jnp.dot(
        spread, pick, preferred_element_type=jnp.float32, precision=lax.Precision.HIGHEST
    )


def sum_sources(received):
    return pl.pallas_call(
        sum_kernel,
        out_shape=jax.ShapeDtypeStruct((8, 32), jnp.float32),
        in_specs=[whole()],
        out_specs=whole(),
        compiler_params=kernel_options(4),
        name="sum_sources",
    )(received).T


def shards(
    fields,
    polarization,
    material,
    omega0,
    damping,
    strength,
    tile_count,
    tile_place,
    dir_angles,
    dir_order,
):
    sizes = tuple(lax.axis_size(axis) * n for axis, n in zip(AXES, fields.shape[1:]))
    index = jnp.stack([lax.axis_index(axis) for axis in AXES]).astype(jnp.int32)
    ints = jnp.concatenate([tile_place.reshape(-1), tile_count.reshape(-1), index])
    medium = jnp.concatenate([omega0, damping, strength])
    fields_out, currents, table, weight = window(
        fields, polarization, material, medium, ints, sizes, dir_angles, dir_order
    )
    tile_total = math.prod(lax.axis_size(axis) for axis in AXES) * TILE_MEAN
    scale = 1.0 / math.sqrt(tile_total * TY * fields.shape[3])
    partial = far_products(currents, table, weight, scale, jnp.bfloat16)
    received = lax.all_to_all(partial, AXES, 0, 0, tiled=True)
    return fields_out, sum_sources(received)


def solution(mesh):
    return jax.shard_map(
        shards,
        mesh=mesh,
        in_specs=(
            P(None, *AXES),
            P(None, *AXES),
            P(*AXES),
            P(),
            P(),
            P(),
            P(("gx", "gy"), None),
            P(("gx", "gy"), None, None),
            P(),
            P(),
        ),
        out_specs=(P(None, *AXES), P(AXES, None)),
        check_vma=False,
    )
```

time: 119 us -> 93.6 us (0.79)
  local copies, waits for them, and re-layouts: 13.4 us -> 3.53 us
  waiting for transfers between devices: 17.1 us -> 7.98 us
  Pallas kernels: 43.2 us -> 36.9 us
    ppermute x6, waiting for transfers between devices: 17.1 us -> 7.98 us  [shift(): return lax.ppermute(block, axis, pairs)]
    unnamed x29 -> x21, local copies, waits for them, and re-layouts: 11.9 us -> 3.21 us
    pallas_call x1, Pallas kernels: 17 us -> 11.7 us  [window(): pl.pallas_call(functools.partial(window_kernel, sizes), out_shape=(jax.Sh...]
    pallas_call x1, Pallas kernels: 7.16 us -> 4.01 us  [directions(): pl.pallas_call(dirs_kernel, out_shape=jax.ShapeDtypeStruct((3, 64, 128),...]
    pallas_call x1, Pallas kernels: 0.71 us -> 2.83 us  [window(): pl.pallas_call(pack_depth_kernel, out_shape=jax.ShapeDtypeStruct((13, 16,...]
    pallas_call x3 -> x5, Pallas kernels: 11.1 us -> 10.7 us  [the longest x1 6.75 us: far_products(): pl.pallas_call(functools.partial(far_kernel, scale), grid=(32 // PER_STEP...]
  transfers between devices with their start and end apart: 6 -> 6, of which waited for: 3 -> 4; matrix products, arithmetic and copies ran while one was open for 2% -> 0% of each run, Pallas kernels for 12% -> 15%
where the time goes in v2:
time: 93.6 us; the launch traced here: 93.2 us
  Pallas kernels  36.9 us (39%)
  blocking collectives  26.4 us (28%)
  starting transfers between devices  17.5 us (19%)
  waiting for transfers between devices  7.98 us (9%)
  local copies, waits for them, and re-layouts  3.53 us (4%)
    all_to_all x1, blocking collectives, shards(): received = lax.all_to_all(partial, AXES, 0, 0, tiled=True)  26.4 us
    ppermute x6, starting transfers between devices, shift(): return lax.ppermute(block, axis, pairs)  17.5 us
    pallas_call x1, Pallas kernels, window(): pl.pallas_call(functools.partial(window_kernel, sizes), out_shape=(jax.Sh...  11.7 us
    ppermute x6, waiting for transfers between devices, shift(): return lax.ppermute(block, axis, pairs)  7.98 us
    pallas_call x1, Pallas kernels, far_products(): pl.pallas_call(functools.partial(far_kernel, scale), grid=(32 // PER_STEP...  6.75 us
    pallas_call x1, Pallas kernels, tables(): pl.pallas_call(tables_kernel, grid=(32,), out_shape=(jax.ShapeDtypeStruct...  6.67 us
    pallas_call x1, Pallas kernels, directions(): pl.pallas_call(dirs_kernel, out_shape=jax.ShapeDtypeStruct((3, 64, 128),...  4.01 us
    unnamed x21, local copies, waits for them, and re-layouts  3.21 us
  transfers between devices with their start and end apart: 6, of which 4 were waited for; matrix products, arithmetic and copies ran while one was open for 0% of the time, Pallas kernels for 15%

profile of v2, /device:TPU:1, one launch (start us, length us, event | category | flops | bytes accessed | tf_op | source)
XLA Modules:
  0.0 93.2 jit_solution(6763864457881623362)
XLA Ops:
  0.6 0.0 copy-start.4
  0.6 0.0 copy-start.3
  0.7 0.0 copy-start.5
  0.7 0.0 copy-start.6
  0.7 2.8 %pack_depth.1 = bf16[13,16,128]{2,1,0:T(8,128)(2,1)} custom-call(f32[6,16,16,128]{3,2,1,0:T(8,128)} %fields_ref.2, f32[6,16,16,128]{3,2,1,0:T(8,128)} %pol_ref.2, s32[16,16,128]{2,1,0:T(8,128)} %mat_ref.2), custom_call_target="tpu_custom_call" | custom-call | tf_op jit(solution)/shard_map/pack_depth/pallas_call | solution.py:381
  3.5 4.9 %collective-permute-start = (bf16[13,16,128]{2,1,0:T(8,128)(2,1)}, bf16[13,16,128]{2,1,0:T(8,128)(2,1)S(1)}, u32[]{:S(2)}, u32[]{:S(2)}) collective-permute-start(bf16[13,16,128]{2,1,0:T(8,128)(2,1)} %pack_depth.1), channel_id=1, source_target_pairs={{0,1},{1,2},{2,3},{4,5},{5,6},{6,7},{8,9},{9,10},{10,11},{12,13},{... | collective-permute-start | bytes 159752 | tf_op jit(solution)/shard_map/ppermute | solution.py:376
  8.4 1.9 %collective-permute-start.1 = (bf16[13,16,128]{2,1,0:T(8,128)(2,1)}, bf16[13,16,128]{2,1,0:T(8,128)(2,1)S(1)}, u32[]{:S(2)}, u32[]{:S(2)}) collective-permute-start(bf16[13,16,128]{2,1,0:T(8,128)(2,1)} %pack_depth.1), channel_id=1, source_target_pairs={{1,0},{2,1},{3,2},{5,4},{6,5},{7,6},{9,8},{10,9},{11,10},{13,12},{... | collective-permute-start | bytes 159752 | tf_op jit(solution)/shard_map/ppermute | solution.py:376
  10.4 0.0 copy-start
  10.4 1.1 %copy-done = f32[6,16,16,128]{3,2,1,0:T(8,128)S(1)} copy-done((f32[6,16,16,128]{3,2,1,0:T(8,128)S(1)}, f32[6,16,16,128]{3,2,1,0:T(8,128)}, u32[]{:S(2)}) %copy-start) | copy-done | bytes 786456
  11.5 0.0 copy-start.1
  11.5 1.1 %copy-done.1 = f32[6,16,16,128]{3,2,1,0:T(8,128)S(1)} copy-done((f32[6,16,16,128]{3,2,1,0:T(8,128)S(1)}, f32[6,16,16,128]{3,2,1,0:T(8,128)}, u32[]{:S(2)}) %copy-start.1) | copy-done | bytes 786456
  12.6 0.0 copy-start.2
  12.6 0.9 copy-done.2
  13.5 0.1 stage.1.own_ref
  13.7 0.0 collective-permute-done.before_ref
  13.7 0.4 collective-permute-done.1.after_ref
  14.1 0.2 pack_x.1
  14.3 4.9 %collective-permute-start.2 = (bf16[48,16,128]{2,1,0:T(8,128)(2,1)S(1)}, bf16[48,16,128]{2,1,0:T(8,128)(2,1)S(1)}, u32[]{:S(2)}, u32[]{:S(2)}) collective-permute-start(bf16[48,16,128]{2,1,0:T(8,128)(2,1)S(1)} %get-tuple-element.18), channel_id=1, source_target_pairs={{0,16},{16,32},{32,48},{48,64},{64,80},{80,96},{96,112},{112,128},... | collective-permute-start | bytes 589832 | tf_op jit(solution)/shard_map/ppermute | solution.py:376
  19.2 1.3 %collective-permute-start.3 = (bf16[45,16,128]{2,1,0:T(8,128)(2,1)S(1)}, bf16[45,16,128]{2,1,0:T(8,128)(2,1)S(1)}, u32[]{:S(2)}, u32[]{:S(2)}) collective-permute-start(bf16[45,16,128]{2,1,0:T(8,128)(2,1)S(1)} %get-tuple-element.19.low_ref), channel_id=1, source_target_pairs={{16,0},{32,16},{48,32},{64,48},{80,64},{96,80},{112,96},{128,112},... | collective-permute-start | bytes 552968 | tf_op jit(solution)/shard_map/ppermute | solution.py:376
  20.5 0.0 copy-done.4
  20.5 0.1 reshape.24
  20.6 0.1 copy.12
  20.7 0.0 copy-start.7
  20.7 0.0 copy-start.8
  20.7 0.0 copy-start.9
  20.7 0.0 copy-done.3
  20.7 0.0 copy-done.5
  20.8 0.1 reshape.21
  20.8 0.0 copy-done.6
  20.8 0.1 concatenate.6.ints_ref
  20.9 4.0 %dirs.1.u_ref = f32[3,64,128]{2,1,0:T(8,128)S(1)} custom-call(f32[2,64,128]{2,1,0:T(8,128)S(1)} %bitcast.13, s32[64,128]{1,0:T(8,128)S(1)} %reshape.25.order_ref, bf16[45,16,128]{2,1,0:T(8,128)(2,1)S(1)} %get-tuple-element.19.low_ref), custom_call_target="tpu_custom_call" | custom-call | flops 3000000 | bytes 300000 | tf_op jit(solution)/shard_map/dirs/pallas_call | solution.py:506
  24.9 6.7 %tables.1 = (bf16[32,512,256]{2,1,0:T(8,128)(2,1)S(1)}, f32[32,2,96,256]{3,2,1,0:T(8,128)S(1)}) custom-call(s32[79]{0:T(128)S(1)} %concatenate.6.ints_ref, bf16[45,16,128]{2,1,0:T(8,128)(2,1)S(1)} %get-tuple-element.19.low_ref, f32[3,64,128]{2,1,0:T(8,128)S(1)} %dirs.1.u_ref), custom_call_target="tpu_custom_call" | custom-call | flops 60000000 | bytes 14000000 | tf_op jit(solution)/shard_map/tables/pallas_call | solution.py:565
  31.6 0.3 collective-permute-done.3.right_ref
  31.9 0.0 collective-permute-done.2.left_ref
  31.9 1.0 %pack_y.1 = (bf16[13,13,8,128]{3,2,1,0:T(8,128)(2,1)S(1)}, bf16[13,13,8,128]{3,2,1,0:T(8,128)(2,1)S(1)}) custom-call(f32[13,16,16,128]{3,2,1,0:T(8,128)S(1)} %stage.1.own_ref, bf16[13,16,128]{2,1,0:T(8,128)(2,1)S(1)} %collective-permute-done.before_ref, bf16[13,16,128]{2,1,0:T(8,128)(2,1)S(1)} %collective-permute-done.1.after_ref, ...), custom_call_target="tpu_custom_call" | custom-call | tf_op jit(solution)/shard_map/pack_y/pallas_call | solution.py:418
  32.9 3.1 %collective-permute-start.4 = (bf16[13,13,8,128]{3,2,1,0:T(8,128)(2,1)S(1)}, bf16[13,13,8,128]{3,2,1,0:T(8,128)(2,1)S(1)}, u32[]{:S(2)}, u32[]{:S(2)}) collective-permute-start(bf16[13,13,8,128]{3,2,1,0:T(8,128)(2,1)S(1)} %get-tuple-element.24), channel_id=1, source_target_pairs={{0,4},{4,8},{8,12},{1,5},{5,9},{9,13},{2,6},{6,10},{10,14},{3,7},{... | collective-permute-start | bytes 1038344 | tf_op jit(solution)/shard_map/ppermute | solution.py:376
  36.0 1.3 %collective-permute-start.5 = (bf16[13,13,8,128]{3,2,1,0:T(8,128)(2,1)S(1)}, bf16[13,13,8,128]{3,2,1,0:T(8,128)(2,1)S(1)}, u32[]{:S(2)}, u32[]{:S(2)}) collective-permute-start(bf16[13,13,8,128]{3,2,1,0:T(8,128)(2,1)S(1)} %get-tuple-element.21.low_ref), channel_id=1, source_target_pairs={{4,0},{8,4},{12,8},{5,1},{9,5},{13,9},{6,2},{10,6},{14,10},{7,3},{... | collective-permute-start | bytes 1038344 | tf_op jit(solution)/shard_map/ppermute | solution.py:376
  37.3 0.0 copy-done.7
  37.3 0.0 copy-done.8
  37.3 0.0 copy-done.9
  37.3 0.1 pad_maximum_fusion.medium_ref
  37.4 2.8 %lay.1 = (f32[12,24,16,256]{3,2,1,0:T(8,128)S(1)}, f32[4,24,16,256]{3,2,1,0:T(8,128)S(1)}) custom-call(f32[12]{0:T(128)S(1)} %pad_maximum_fusion.medium_ref, f32[13,16,16,128]{3,2,1,0:T(8,128)S(1)} %stage.1.own_ref, bf16[13,16,128]{2,1,0:T(8,128)(2,1)S(1)} %collective-permute-done.before_ref, bf16[13,16,128]{2,1,0:T(8,128)(2,1)S(1)} %collective-permute-done.1.after_ref, ...), custom_call_target="tpu_custom_call" | custom-call | flops 8000000 | bytes 9000000 | tf_op jit(solution)/shard_map/lay/pallas_call | solution.py:426
  40.2 3.4 %collective-permute-done.4.down_ref = bf16[13,13,8,128]{3,2,1,0:T(8,128)(2,1)S(1)} collective-permute-done((bf16[13,13,8,128]{3,2,1,0:T(8,128)(2,1)S(1)}, bf16[13,13,8,128]{3,2,1,0:T(8,128)(2,1)S(1)}, u32[]{:S(2)}, u32[]{:S(2)}) %collective-permute-start.4) | collective-permute-done | bytes 346144 | tf_op jit(solution)/shard_map/ppermute | solution.py:376
  43.6 3.9 %collective-permute-done.5.up_ref = bf16[13,13,8,128]{3,2,1,0:T(8,128)(2,1)S(1)} collective-permute-done((bf16[13,13,8,128]{3,2,1,0:T(8,128)(2,1)S(1)}, bf16[13,13,8,128]{3,2,1,0:T(8,128)(2,1)S(1)}, u32[]{:S(2)}, u32[]{:S(2)}) %collective-permute-start.5) | collective-permute-done | bytes 346144 | tf_op jit(solution)/shard_map/ppermute | solution.py:376
  47.5 11.7 %window.1 = (f32[6,16,16,128]{3,2,1,0:T(8,128)}, f32[1152,128]{1,0:T(8,128)S(1)}) custom-call(s32[79]{0:T(128)S(1)} %concatenate.6.ints_ref, f32[12]{0:T(128)S(1)} %pad_maximum_fusion.medium_ref, f32[12,24,16,256]{3,2,1,0:T(8,128)S(1)} %get-tuple-element.22.laid_ref, f32[4,24,16,256]{3,2,1,0:T(8,128)S(1)} %get-tuple-element.23.laid_coef_ref, ...), custom_call_target="tpu_custom_call" | custom-call | tf_op jit(solution)/shard_map/window/pallas_call | solution.py:439
  59.2 6.7 %far.1 = bf16[512,128]{1,0:T(8,128)(2,1)S(1)} custom-call(f32[1152,128]{1,0:T(8,128)S(1)} %get-tuple-element.26.cur_ref, bf16[32,512,256]{2,1,0:T(8,128)(2,1)S(1)} %get-tuple-element.27.table_ref, f32[32,2,96,256]{3,2,1,0:T(8,128)S(1)} %get-tuple-element.20.u_ref.weight_ref), custom_call_target="tpu_custom_call" | custom-call | flops 5000000000 | bytes 15000000 | tf_op jit(solution)/shard_map/far/pallas_call | solution.py:628
  66.0 26.4 %all_to_all.11 = bf16[256,2,128]{2,1,0:T(2,128)(2,1)S(1)} all-to-all(bf16[256,2,128]{2,1,0:T(2,128)(2,1)S(1)} %bitcast.14), channel_id=1, replica_groups=mesh['gx'=16,'gy'=4,'gz'=4] {'gx','gy','gz'}, dimensions={0} | all-to-all | bytes 262144 | tf_op jit(solution)/shard_map/all_to_all | solution.py:700
  92.4 0.9 sum_sources.1
  (2 shorter events, 0.0 us)
Async XLA Ops:
  0.6 19.9 %copy-start.4 = (s32[8192]{0:T(1024)S(1)}, s32[8192]{0:T(1024)}, u32[]{:S(2)}) copy-start(s32[8192]{0:T(1024)} %param.19) | copy-start | bytes 98308
  0.6 20.1 %copy-start.3 = (f32[2,8192]{1,0:T(2,128)S(1)}, f32[2,8192]{1,0:T(2,128)}, u32[]{:S(2)}) copy-start(f32[2,8192]{1,0:T(2,128)} %param.18) | copy-start | bytes 196612
  0.7 20.1 %copy-start.5 = (s32[1,4,18]{2,1,0:T(4,128)S(1)}, s32[1,4,18]{2,1,0:T(4,128)}, u32[]{:S(2)}) copy-start(s32[1,4,18]{2,1,0:T(4,128)} %param.17) | copy-start | bytes 868
  0.7 20.2 %copy-start.6 = (s32[1,4]{1,0:T(1,128)S(1)}, s32[1,4]{1,0:T(1,128)}, u32[]{:S(2)}) copy-start(s32[1,4]{1,0:T(1,128)} %param.16) | copy-start | bytes 52
  3.5 10.2 %collective-permute-start = (bf16[13,16,128]{2,1,0:T(8,128)(2,1)}, bf16[13,16,128]{2,1,0:T(8,128)(2,1)S(1)}, u32[]{:S(2)}, u32[]{:S(2)}) collective-permute-start(bf16[13,16,128]{2,1,0:T(8,128)(2,1)} %pack_depth.1), channel_id=1, source_target_pairs={{0,1},{1,2},{2,3},{4,5},{5,6},{6,7},{8,9},{9,10},{10,11},{12,13},{... | collective-permute-start | bytes 159752 | tf_op jit(solution)/shard_map/ppermute | solution.py:376
  8.4 5.7 %collective-permute-start.1 = (bf16[13,16,128]{2,1,0:T(8,128)(2,1)}, bf16[13,16,128]{2,1,0:T(8,128)(2,1)S(1)}, u32[]{:S(2)}, u32[]{:S(2)}) collective-permute-start(bf16[13,16,128]{2,1,0:T(8,128)(2,1)} %pack_depth.1), channel_id=1, source_target_pairs={{1,0},{2,1},{3,2},{5,4},{6,5},{7,6},{9,8},{10,9},{11,10},{13,12},{... | collective-permute-start | bytes 159752 | tf_op jit(solution)/shard_map/ppermute | solution.py:376
  10.4 1.1 %copy-start = (f32[6,16,16,128]{3,2,1,0:T(8,128)S(1)}, f32[6,16,16,128]{3,2,1,0:T(8,128)}, u32[]{:S(2)}) copy-start(f32[6,16,16,128]{3,2,1,0:T(8,128)} %fields_ref.2) | copy-start | bytes 2359300
  11.5 1.1 %copy-start.1 = (f32[6,16,16,128]{3,2,1,0:T(8,128)S(1)}, f32[6,16,16,128]{3,2,1,0:T(8,128)}, u32[]{:S(2)}) copy-start(f32[6,16,16,128]{3,2,1,0:T(8,128)} %pol_ref.2) | copy-start | bytes 2359300
  12.6 0.9 copy-start.2
  14.3 17.6 %collective-permute-start.2 = (bf16[48,16,128]{2,1,0:T(8,128)(2,1)S(1)}, bf16[48,16,128]{2,1,0:T(8,128)(2,1)S(1)}, u32[]{:S(2)}, u32[]{:S(2)}) collective-permute-start(bf16[48,16,128]{2,1,0:T(8,128)(2,1)S(1)} %get-tuple-element.18), channel_id=1, source_target_pairs={{0,16},{16,32},{32,48},{48,64},{64,80},{80,96},{96,112},{112,128},... | collective-permute-start | bytes 589832 | tf_op jit(solution)/shard_map/ppermute | solution.py:376
  19.2 12.7 %collective-permute-start.3 = (bf16[45,16,128]{2,1,0:T(8,128)(2,1)S(1)}, bf16[45,16,128]{2,1,0:T(8,128)(2,1)S(1)}, u32[]{:S(2)}, u32[]{:S(2)}) collective-permute-start(bf16[45,16,128]{2,1,0:T(8,128)(2,1)S(1)} %get-tuple-element.19.low_ref), channel_id=1, source_target_pairs={{16,0},{32,16},{48,32},{64,48},{80,64},{96,80},{112,96},{128,112},... | collective-permute-start | bytes 552968 | tf_op jit(solution)/shard_map/ppermute | solution.py:376
  20.7 16.6 %copy-start.7 = (f32[4]{0:T(128)S(1)}, f32[4]{0:T(128)}, u32[]{:S(2)}) copy-start(f32[4]{0:T(128)} %param.15) | copy-start | bytes 52
  20.7 16.7 %copy-start.8 = (f32[4]{0:T(128)S(1)}, f32[4]{0:T(128)}, u32[]{:S(2)}) copy-start(f32[4]{0:T(128)} %param.14) | copy-start | bytes 52
  20.7 16.6 %copy-start.9 = (f32[4]{0:T(128)S(1)}, f32[4]{0:T(128)}, u32[]{:S(2)}) copy-start(f32[4]{0:T(128)} %param.13) | copy-start | bytes 52
  32.9 10.8 %collective-permute-start.4 = (bf16[13,13,8,128]{3,2,1,0:T(8,128)(2,1)S(1)}, bf16[13,13,8,128]{3,2,1,0:T(8,128)(2,1)S(1)}, u32[]{:S(2)}, u32[]{:S(2)}) collective-permute-start(bf16[13,13,8,128]{3,2,1,0:T(8,128)(2,1)S(1)} %get-tuple-element.24), channel_id=1, source_target_pairs={{0,4},{4,8},{8,12},{1,5},{5,9},{9,13},{2,6},{6,10},{10,14},{3,7},{... | collective-permute-start | bytes 1038344 | tf_op jit(solution)/shard_map/ppermute | solution.py:376
  36.0 11.5 %collective-permute-start.5 = (bf16[13,13,8,128]{3,2,1,0:T(8,128)(2,1)S(1)}, bf16[13,13,8,128]{3,2,1,0:T(8,128)(2,1)S(1)}, u32[]{:S(2)}, u32[]{:S(2)}) collective-permute-start(bf16[13,13,8,128]{3,2,1,0:T(8,128)(2,1)S(1)} %get-tuple-element.21.low_ref), channel_id=1, source_target_pairs={{4,0},{8,4},{12,8},{5,1},{9,5},{13,9},{6,2},{10,6},{14,10},{7,3},{... | collective-permute-start | bytes 1038344 | tf_op jit(solution)/shard_map/ppermute | solution.py:376

commit v3 on v2

--- a/solution.py
+++ b/solution.py
@@ -15,8 +15,8 @@
 SPEED = 0.5
 WAVE = 0.35
 HALO = jnp.bfloat16
-BLOCK = 8
-PER_STEP = 4
+LAG = 4
+PER_STEP = 8
 AXES = ("gx", "gy", "gz")
 
 
@@ -87,9 +87,9 @@
     if x < 19:
         return right_ref[a * 3 + x - 16].astype(jnp.float32)
     if x == 19:
-        return right_ref[39 + jnp.clip(a - 1, 0, 1)].astype(jnp.float32)
+        return right_ref[39 + min(max(a - 1, 0), 1)].astype(jnp.float32)
     if x == 20:
-        return left_ref[39 + jnp.minimum(jnp.where(a < 3, a, a - 1), 4)].astype(jnp.float32)
+        return left_ref[39 + min(a if a < 3 else a - 1, 4)].astype(jnp.float32)
     if x < 24:
         return left_ref[a * 3 + x - 21].astype(jnp.float32)
     if x == 24:
@@ -108,7 +108,7 @@
 ):
     top = lax.broadcasted_iota(jnp.int32, (8, 128), 0) < 4
 
-    def body(a, carry):
+    for a in range(13):
         for i in range(13):
             p0, p1 = [
                 wide_plane(2 * i + k, a, own_ref, before_ref, after_ref, left_ref, right_ref)
@@ -116,9 +116,6 @@
             ]
             low_ref[a, i] = jnp.where(top, p0[0:8], pltpu.roll(p1[0:8], 4, 0)).astype(HALO)
             high_ref[a, i] = jnp.where(top, pltpu.roll(p1[8:16], 4, 0), p0[8:16]).astype(HALO)
-        return carry
-
-    lax.fori_loop(0, 13, body, 0)
 
 
 def side_lanes(depth, x):
@@ -155,20 +152,18 @@
             main = wide_plane(x, a, own_ref, before_ref, after_ref, left_ref, right_ref)
             store(x, jnp.concatenate([main, side_lanes(depth, x)], axis=1))
 
-    def body(a, carry):
-        def store(x, value):
+    for a in range(12):
+
+        def store(x, value, a=a):
             wide_ref[a, x] = value
 
         spread(a, store)
-        return carry
-
-    lax.fori_loop(0, 12, body, 0)
 
     def store_coef(x, value):
         for k, coef in enumerate(coefficients(medium_ref, value)):
             coef_ref[k, x] = coef
 
-    spread(jnp.int32(12), store_coef)
+    spread(12, store_coef)
 
 
 def window_kernel(
@@ -185,6 +180,8 @@
     tail_ref,
     tail_coef_ref,
     phasor_ref,
+    final_ref,
+    sems,
 ):
     top = lax.broadcasted_iota(jnp.int32, (8, 128), 0) < 4
 
@@ -204,14 +201,12 @@
                 x = 2 * i + k
                 store(x, jnp.concatenate([tail[k], side_lanes(depth, x)], axis=1))
 
-    def body(a, carry):
-        def store(x, value):
+    for a in range(12):
+
+        def store(x, value, a=a):
             tail_ref[a, x] = value
 
         spread(a, store)
-        return carry
-
-    lax.fori_loop(0, 12, body, 0)
 
     def store_coef(x, value):
         for k, coef in enumerate(coefficients(medium_ref, value)):
@@ -246,13 +241,18 @@
     def behind_z(v):
         return pltpu.roll(v, 1, 1)
 
+    for k in (4, 5):
+        wide_ref[k, 19] = jnp.zeros((24, 256), jnp.float32)
+
     def wrap(x):
-        return jnp.where(x < 0, x + 24, x) if not isinstance(x, int) else x % 24
+        return x % 24
 
     def magnetic_step(n, x):
         here, after = wrap(x), wrap(x + 1)
         place = gx * 16 + x
-        speed = inside * jnp.where((place >= 0) & (place < extents[0]), 1.0, 0.0)
+        speed = inside
+        if not 0 <= x < 16:
+            speed = inside * jnp.where((place >= 0) & (place < extents[0]), 1.0, 0.0)
         get = first_value if n == 0 else (lambda k, at: wide_ref[k, at])
         ex, ey, ez = get(0, here), get(1, here), get(2, here)
         ey_next, ez_next = get(1, after), get(2, after)
@@ -305,7 +305,7 @@
             pol_new = a * pol + b * get(old + c, here) + drive * e
             value = e + rate * curls[c] - sheet * (pol_new - pol)
             if last:
-                out_ref[c, x] = value
+                final_ref[c, x] = value
             else:
                 put(old + c, pol_new)
                 put(c, value)
@@ -328,30 +328,30 @@
             for o, (factor, value) in enumerate(terms):
                 phasor_ref[o, x] = factor * value if n == 0 else phasor_ref[o, x] + factor * value
             if last:
-                out_ref[3, x] = hxc
-                out_ref[4, x] = hyc
-                out_ref[5, x] = hzc
-
-    def block_step(n, first, count, inner):
-        states = [magnetic_step(n, first + k) for k in range(count)]
-        if n == STEPS - 1 and not inner:
-            return
-        for k, state in enumerate(states):
-            electric_step(n, first + k, inner, *state)
-
-    for k in (4, 5):
-        wide_ref[k, 19] = jnp.zeros((24, 256), jnp.float32)
-
+                final_ref[3, x] = hxc
+                final_ref[4, x] = hyc
+                final_ref[5, x] = hzc
+
+    copies = []
     for n in range(STEPS):
-        block_step(n, n - 4, 4 - n, False)
-
-        def step(i, carry, n=n):
-            block_step(n, i * BLOCK, BLOCK, True)
-            return carry
-
-        lax.fori_loop(0, 16 // BLOCK, step, 0)
-        if n < STEPS - 1:
-            block_step(n, 16, 3 - n, False)
+        planes = list(range(n - 4, 19 - n))
+        states = {}
+        for k in range(len(planes) + LAG):
+            if k < len(planes):
+                states[planes[k]] = magnetic_step(n, planes[k])
+            if k >= LAG:
+                x = planes[k - LAG]
+                inner = 0 <= x < 16
+                if inner or n < STEPS - 1:
+                    electric_step(n, x, inner, *states.pop(x))
+                if n == STEPS - 1 and inner and x % 4 == 3:
+                    part = pl.ds(x - 3, 4)
+                    copies.append(
+                        pltpu.make_async_copy(
+                            final_ref.at[:, part], out_ref.at[:, part], sems.at[x // 4]
+                        )
+                    )
+                    copies[-1].start()
 
     count = ints_ref[72 + gz]
 
@@ -364,6 +364,8 @@
         return carry
 
     lax.fori_loop(0, SLOTS, put_tile, 0)
+    for copy in copies:
+        copy.wait()
 
 
 def kernel_options(mib):
@@ -443,12 +445,14 @@
             jax.ShapeDtypeStruct((SLOTS * 64, 128), jnp.float32),
         ),
         in_specs=[scalars()] * 2 + [whole()] * 4,
-        out_specs=(whole(),) * 2,
+        out_specs=(anywhere, whole()),
         scratch_shapes=[
             pltpu.VMEM((12, 24, 24, 256), jnp.float32),
             pltpu.VMEM((12, 24, 8, 256), jnp.float32),
             pltpu.VMEM((4, 24, 8, 256), jnp.float32),
             pltpu.VMEM((8, 16, 16, 128), jnp.float32),
+            pltpu.VMEM((6, 16, 16, 128), jnp.float32),
+            pltpu.SemaphoreType.DMA((4,)),
         ],
         compiler_params=kernel_options(24),
         name="window",
@@ -567,7 +571,7 @@
         grid=(32,),
         out_shape=(
             jax.ShapeDtypeStruct((32, 512, 256), jnp.bfloat16),
-            jax.ShapeDtypeStruct((32, 2, 96, 256), jnp.float32),
+            jax.ShapeDtypeStruct((32, 2, 104, 256), jnp.float32),
         ),
         in_specs=[
             scalars(),
@@ -576,7 +580,7 @@
         ],
         out_specs=(
             pl.BlockSpec((1, 512, 256), lambda j: (j, 0, 0)),
-            pl.BlockSpec((1, 2, 96, 256), lambda j: (j, 0, 0, 0)),
+            pl.BlockSpec((1, 2, 104, 256), lambda j: (j, 0, 0, 0)),
         ),
         scratch_shapes=[pltpu.VMEM((3, 24, 256), jnp.float32)],
         cost_estimate=pl.CostEstimate(flops=60000000, bytes_accessed=14000000, transcendentals=0),
@@ -632,7 +636,7 @@
         in_specs=[
             pl.BlockSpec((SLOTS * 64, 128), lambda j: (0, 0)),
             pl.BlockSpec((PER_STEP, 512, 256), lambda j: (j, 0, 0)),
-            pl.BlockSpec((PER_STEP, 2, 96, 256), lambda j: (j, 0, 0, 0)),
+            pl.BlockSpec((PER_STEP, 2, 104, 256), lambda j: (j, 0, 0, 0)),
         ],
         out_specs=pl.BlockSpec((512, 128), lambda j: (0, 0)),
         scratch_shapes=[

time: 93.6 us -> 86.9 us (0.928)
  Pallas kernels: 36.9 us -> 29.1 us
  waiting for transfers between devices: 7.98 us -> 8.95 us
    pallas_call x1, Pallas kernels: 11.7 us -> 6.4 us  [window(): pl.pallas_call(functools.partial(window_kernel, sizes), out_shape=(jax.Sh...]
    pallas_call x1, Pallas kernels: 2.78 us -> 1.8 us  [window(): pl.pallas_call(lay_kernel, out_shape=(jax.ShapeDtypeStruct((12, 24, 16, 2...]
    ppermute x6, waiting for transfers between devices: 7.98 us -> 8.95 us  [shift(): return lax.ppermute(block, axis, pairs)]
where the time goes in v3:
time: 86.9 us; the launch traced here: 86.5 us
  Pallas kernels  29.1 us (33%)
  blocking collectives  26.4 us (30%)
  starting transfers between devices  17.5 us (20%)
  waiting for transfers between devices  8.95 us (10%)
  local copies, waits for them, and re-layouts  3.53 us (4%)
  between operations  0.9 us (1%)
    all_to_all x1, blocking collectives, shards(): received = lax.all_to_all(partial, AXES, 0, 0, tiled=True)  26.4 us
    ppermute x6, starting transfers between devices, shift(): return lax.ppermute(block, axis, pairs)  17.5 us
    ppermute x6, waiting for transfers between devices, shift(): return lax.ppermute(block, axis, pairs)  8.95 us
    pallas_call x1, Pallas kernels, tables(): pl.pallas_call(tables_kernel, grid=(32,), out_shape=(jax.ShapeDtypeStruct...  6.67 us
    pallas_call x1, Pallas kernels, window(): pl.pallas_call(functools.partial(window_kernel, sizes), out_shape=(jax.Sh...  6.4 us
    pallas_call x1, Pallas kernels, far_products(): pl.pallas_call(functools.partial(far_kernel, scale), grid=(32 // PER_STEP...  6.08 us
    pallas_call x1, Pallas kernels, directions(): pl.pallas_call(dirs_kernel, out_shape=jax.ShapeDtypeStruct((3, 64, 128),...  4.01 us
    unnamed x21, local copies, waits for them, and re-layouts  3.21 us
  transfers between devices with their start and end apart: 6, of which 4 were waited for; matrix products, arithmetic and copies ran while one was open for 0% of the time, Pallas kernels for 15%

profile of v3, /device:TPU:1, one launch (start us, length us, event | category | flops | bytes accessed | tf_op | source)
XLA Modules:
  0.0 86.5 jit_solution(6750715726826283540)
XLA Ops:
  0.6 0.0 copy-start.4
  0.6 0.0 copy-start.3
  0.7 0.0 copy-start.5
  0.7 0.0 copy-start.6
  0.7 2.8 %pack_depth.1 = bf16[13,16,128]{2,1,0:T(8,128)(2,1)} custom-call(f32[6,16,16,128]{3,2,1,0:T(8,128)} %fields_ref.2, f32[6,16,16,128]{3,2,1,0:T(8,128)} %pol_ref.2, s32[16,16,128]{2,1,0:T(8,128)} %mat_ref.2), custom_call_target="tpu_custom_call" | custom-call | tf_op jit(solution)/shard_map/pack_depth/pallas_call | solution.py:383
  3.5 4.9 %collective-permute-start = (bf16[13,16,128]{2,1,0:T(8,128)(2,1)}, bf16[13,16,128]{2,1,0:T(8,128)(2,1)S(1)}, u32[]{:S(2)}, u32[]{:S(2)}) collective-permute-start(bf16[13,16,128]{2,1,0:T(8,128)(2,1)} %pack_depth.1), channel_id=1, source_target_pairs={{0,1},{1,2},{2,3},{4,5},{5,6},{6,7},{8,9},{9,10},{10,11},{12,13},{... | collective-permute-start | bytes 159752 | tf_op jit(solution)/shard_map/ppermute | solution.py:378
  8.4 1.9 %collective-permute-start.1 = (bf16[13,16,128]{2,1,0:T(8,128)(2,1)}, bf16[13,16,128]{2,1,0:T(8,128)(2,1)S(1)}, u32[]{:S(2)}, u32[]{:S(2)}) collective-permute-start(bf16[13,16,128]{2,1,0:T(8,128)(2,1)} %pack_depth.1), channel_id=1, source_target_pairs={{1,0},{2,1},{3,2},{5,4},{6,5},{7,6},{9,8},{10,9},{11,10},{13,12},{... | collective-permute-start | bytes 159752 | tf_op jit(solution)/shard_map/ppermute | solution.py:378
  10.4 0.0 copy-start
  10.4 1.1 %copy-done = f32[6,16,16,128]{3,2,1,0:T(8,128)S(1)} copy-done((f32[6,16,16,128]{3,2,1,0:T(8,128)S(1)}, f32[6,16,16,128]{3,2,1,0:T(8,128)}, u32[]{:S(2)}) %copy-start) | copy-done | bytes 786456
  11.5 0.0 copy-start.1
  11.5 1.1 %copy-done.1 = f32[6,16,16,128]{3,2,1,0:T(8,128)S(1)} copy-done((f32[6,16,16,128]{3,2,1,0:T(8,128)S(1)}, f32[6,16,16,128]{3,2,1,0:T(8,128)}, u32[]{:S(2)}) %copy-start.1) | copy-done | bytes 786456
  12.6 0.0 copy-start.2
  12.6 0.9 %copy-done.2 = s32[16,16,128]{2,1,0:T(8,128)S(1)} copy-done((s32[16,16,128]{2,1,0:T(8,128)S(1)}, s32[16,16,128]{2,1,0:T(8,128)}, u32[]{:S(2)}) %copy-start.2) | copy-done | bytes 131096
  13.5 0.1 stage.1.own_ref
  13.7 0.0 collective-permute-done.before_ref
  13.7 0.4 collective-permute-done.1.after_ref
  14.1 0.2 pack_x.1
  14.3 4.9 %collective-permute-start.2 = (bf16[48,16,128]{2,1,0:T(8,128)(2,1)S(1)}, bf16[48,16,128]{2,1,0:T(8,128)(2,1)S(1)}, u32[]{:S(2)}, u32[]{:S(2)}) collective-permute-start(bf16[48,16,128]{2,1,0:T(8,128)(2,1)S(1)} %get-tuple-element.18), channel_id=1, source_target_pairs={{0,16},{16,32},{32,48},{48,64},{64,80},{80,96},{96,112},{112,128},... | collective-permute-start | bytes 589832 | tf_op jit(solution)/shard_map/ppermute | solution.py:378
  19.2 1.3 %collective-permute-start.3 = (bf16[45,16,128]{2,1,0:T(8,128)(2,1)S(1)}, bf16[45,16,128]{2,1,0:T(8,128)(2,1)S(1)}, u32[]{:S(2)}, u32[]{:S(2)}) collective-permute-start(bf16[45,16,128]{2,1,0:T(8,128)(2,1)S(1)} %get-tuple-element.19.low_ref), channel_id=1, source_target_pairs={{16,0},{32,16},{48,32},{64,48},{80,64},{96,80},{112,96},{128,112},... | collective-permute-start | bytes 552968 | tf_op jit(solution)/shard_map/ppermute | solution.py:378
  20.5 0.0 copy-done.4
  20.5 0.1 reshape.24
  20.6 0.1 copy.12
  20.7 0.0 copy-done.3
  20.7 0.0 copy-done.5
  20.7 0.1 reshape.21
  20.8 0.0 copy-done.6
  20.8 0.1 concatenate.6.ints_ref
  20.9 4.0 %dirs.1.u_ref = f32[3,64,128]{2,1,0:T(8,128)S(1)} custom-call(f32[2,64,128]{2,1,0:T(8,128)S(1)} %bitcast.13, s32[64,128]{1,0:T(8,128)S(1)} %reshape.25.order_ref, bf16[45,16,128]{2,1,0:T(8,128)(2,1)S(1)} %get-tuple-element.19.low_ref), custom_call_target="tpu_custom_call" | custom-call | flops 3000000 | bytes 300000 | tf_op jit(solution)/shard_map/dirs/pallas_call | solution.py:510
  24.9 0.0 copy-start.7
  24.9 0.0 copy-start.8
  24.9 0.0 copy-start.9
  24.9 6.7 %tables.1 = (bf16[32,512,256]{2,1,0:T(8,128)(2,1)S(1)}, f32[32,2,104,256]{3,2,1,0:T(8,128)S(1)}) custom-call(s32[79]{0:T(128)S(1)} %concatenate.6.ints_ref, bf16[45,16,128]{2,1,0:T(8,128)(2,1)S(1)} %get-tuple-element.19.low_ref, f32[3,64,128]{2,1,0:T(8,128)S(1)} %dirs.1.u_ref), custom_call_target="tpu_custom_call" | custom-call | flops 60000000 | bytes 14000000 | tf_op jit(solution)/shard_map/tables/pallas_call | solution.py:569
  31.6 0.2 collective-permute-done.3.right_ref
  31.9 0.0 collective-permute-done.2.left_ref
  31.9 0.2 pack_y.1
  32.1 3.1 %collective-permute-start.4 = (bf16[13,13,8,128]{3,2,1,0:T(8,128)(2,1)S(1)}, bf16[13,13,8,128]{3,2,1,0:T(8,128)(2,1)S(1)}, u32[]{:S(2)}, u32[]{:S(2)}) collective-permute-start(bf16[13,13,8,128]{3,2,1,0:T(8,128)(2,1)S(1)} %get-tuple-element.24), channel_id=1, source_target_pairs={{0,4},{4,8},{8,12},{1,5},{5,9},{9,13},{2,6},{6,10},{10,14},{3,7},{... | collective-permute-start | bytes 1038344 | tf_op jit(solution)/shard_map/ppermute | solution.py:378
  35.2 1.3 %collective-permute-start.5 = (bf16[13,13,8,128]{3,2,1,0:T(8,128)(2,1)S(1)}, bf16[13,13,8,128]{3,2,1,0:T(8,128)(2,1)S(1)}, u32[]{:S(2)}, u32[]{:S(2)}) collective-permute-start(bf16[13,13,8,128]{3,2,1,0:T(8,128)(2,1)S(1)} %get-tuple-element.21.low_ref), channel_id=1, source_target_pairs={{4,0},{8,4},{12,8},{5,1},{9,5},{13,9},{6,2},{10,6},{14,10},{7,3},{... | collective-permute-start | bytes 1038344 | tf_op jit(solution)/shard_map/ppermute | solution.py:378
  36.5 0.0 copy-done.7
  36.5 0.0 copy-done.8
  36.5 0.0 copy-done.9
  36.6 0.1 pad_maximum_fusion.medium_ref
  36.6 1.8 %lay.1 = (f32[12,24,16,256]{3,2,1,0:T(8,128)S(1)}, f32[4,24,16,256]{3,2,1,0:T(8,128)S(1)}) custom-call(f32[12]{0:T(128)S(1)} %pad_maximum_fusion.medium_ref, f32[13,16,16,128]{3,2,1,0:T(8,128)S(1)} %stage.1.own_ref, bf16[13,16,128]{2,1,0:T(8,128)(2,1)S(1)} %collective-permute-done.before_ref, bf16[13,16,128]{2,1,0:T(8,128)(2,1)S(1)} %collective-permute-done.1.after_ref, ...), custom_call_target="tpu_custom_call" | custom-call | flops 8000000 | bytes 9000000 | tf_op jit(solution)/shard_map/lay/pallas_call | solution.py:428
  38.4 4.4 %collective-permute-done.4.down_ref = bf16[13,13,8,128]{3,2,1,0:T(8,128)(2,1)S(1)} collective-permute-done((bf16[13,13,8,128]{3,2,1,0:T(8,128)(2,1)S(1)}, bf16[13,13,8,128]{3,2,1,0:T(8,128)(2,1)S(1)}, u32[]{:S(2)}, u32[]{:S(2)}) %collective-permute-start.4) | collective-permute-done | bytes 346144 | tf_op jit(solution)/shard_map/ppermute | solution.py:378
  42.8 3.9 %collective-permute-done.5.up_ref = bf16[13,13,8,128]{3,2,1,0:T(8,128)(2,1)S(1)} collective-permute-done((bf16[13,13,8,128]{3,2,1,0:T(8,128)(2,1)S(1)}, bf16[13,13,8,128]{3,2,1,0:T(8,128)(2,1)S(1)}, u32[]{:S(2)}, u32[]{:S(2)}) %collective-permute-start.5) | collective-permute-done | bytes 346144 | tf_op jit(solution)/shard_map/ppermute | solution.py:378
  46.7 6.4 %window.1 = (f32[6,16,16,128]{3,2,1,0:T(8,128)}, f32[1152,128]{1,0:T(8,128)S(1)}) custom-call(s32[79]{0:T(128)S(1)} %concatenate.6.ints_ref, f32[12]{0:T(128)S(1)} %pad_maximum_fusion.medium_ref, f32[12,24,16,256]{3,2,1,0:T(8,128)S(1)} %get-tuple-element.22.laid_ref, f32[4,24,16,256]{3,2,1,0:T(8,128)S(1)} %get-tuple-element.23.laid_coef_ref, ...), custom_call_target="tpu_custom_call" | custom-call | tf_op jit(solution)/shard_map/window/pallas_call | solution.py:441
  53.1 6.1 %far.1 = bf16[512,128]{1,0:T(8,128)(2,1)S(1)} custom-call(f32[1152,128]{1,0:T(8,128)S(1)} %get-tuple-element.26.cur_ref, bf16[32,512,256]{2,1,0:T(8,128)(2,1)S(1)} %get-tuple-element.27.table_ref, f32[32,2,104,256]{3,2,1,0:T(8,128)S(1)} %get-tuple-element.20.u_ref.weight_ref), custom_call_target="tpu_custom_call" | custom-call | flops 5000000000 | bytes 15000000 | tf_op jit(solution)/shard_map/far/pallas_call | solution.py:632
  59.2 26.4 %all_to_all.11 = bf16[256,2,128]{2,1,0:T(2,128)(2,1)S(1)} all-to-all(bf16[256,2,128]{2,1,0:T(2,128)(2,1)S(1)} %bitcast.14), channel_id=1, replica_groups=mesh['gx'=16,'gy'=4,'gz'=4] {'gx','gy','gz'}, dimensions={0} | all-to-all | bytes 262144 | tf_op jit(solution)/shard_map/all_to_all | solution.py:704
  85.6 0.9 sum_sources.1
  (2 shorter events, 0.0 us)
Async XLA Ops:
  0.6 19.9 %copy-start.4 = (s32[8192]{0:T(1024)S(1)}, s32[8192]{0:T(1024)}, u32[]{:S(2)}) copy-start(s32[8192]{0:T(1024)} %param.19) | copy-start | bytes 98308
  0.6 20.0 %copy-start.3 = (f32[2,8192]{1,0:T(2,128)S(1)}, f32[2,8192]{1,0:T(2,128)}, u32[]{:S(2)}) copy-start(f32[2,8192]{1,0:T(2,128)} %param.18) | copy-start | bytes 196612
  0.7 20.1 %copy-start.5 = (s32[1,4,18]{2,1,0:T(4,128)S(1)}, s32[1,4,18]{2,1,0:T(4,128)}, u32[]{:S(2)}) copy-start(s32[1,4,18]{2,1,0:T(4,128)} %param.17) | copy-start | bytes 868
  0.7 20.2 %copy-start.6 = (s32[1,4]{1,0:T(1,128)S(1)}, s32[1,4]{1,0:T(1,128)}, u32[]{:S(2)}) copy-start(s32[1,4]{1,0:T(1,128)} %param.16) | copy-start | bytes 52
  3.5 10.2 %collective-permute-start = (bf16[13,16,128]{2,1,0:T(8,128)(2,1)}, bf16[13,16,128]{2,1,0:T(8,128)(2,1)S(1)}, u32[]{:S(2)}, u32[]{:S(2)}) collective-permute-start(bf16[13,16,128]{2,1,0:T(8,128)(2,1)} %pack_depth.1), channel_id=1, source_target_pairs={{0,1},{1,2},{2,3},{4,5},{5,6},{6,7},{8,9},{9,10},{10,11},{12,13},{... | collective-permute-start | bytes 159752 | tf_op jit(solution)/shard_map/ppermute | solution.py:378
  8.4 5.7 %collective-permute-start.1 = (bf16[13,16,128]{2,1,0:T(8,128)(2,1)}, bf16[13,16,128]{2,1,0:T(8,128)(2,1)S(1)}, u32[]{:S(2)}, u32[]{:S(2)}) collective-permute-start(bf16[13,16,128]{2,1,0:T(8,128)(2,1)} %pack_depth.1), channel_id=1, source_target_pairs={{1,0},{2,1},{3,2},{5,4},{6,5},{7,6},{9,8},{10,9},{11,10},{13,12},{... | collective-permute-start | bytes 159752 | tf_op jit(solution)/shard_map/ppermute | solution.py:378
  10.4 1.1 %copy-start = (f32[6,16,16,128]{3,2,1,0:T(8,128)S(1)}, f32[6,16,16,128]{3,2,1,0:T(8,128)}, u32[]{:S(2)}) copy-start(f32[6,16,16,128]{3,2,1,0:T(8,128)} %fields_ref.2) | copy-start | bytes 2359300
  11.5 1.1 %copy-start.1 = (f32[6,16,16,128]{3,2,1,0:T(8,128)S(1)}, f32[6,16,16,128]{3,2,1,0:T(8,128)}, u32[]{:S(2)}) copy-start(f32[6,16,16,128]{3,2,1,0:T(8,128)} %pol_ref.2) | copy-start | bytes 2359300
  12.6 0.9 %copy-start.2 = (s32[16,16,128]{2,1,0:T(8,128)S(1)}, s32[16,16,128]{2,1,0:T(8,128)}, u32[]{:S(2)}) copy-start(s32[16,16,128]{2,1,0:T(8,128)} %mat_ref.2) | copy-start | bytes 393220
  14.3 17.6 %collective-permute-start.2 = (bf16[48,16,128]{2,1,0:T(8,128)(2,1)S(1)}, bf16[48,16,128]{2,1,0:T(8,128)(2,1)S(1)}, u32[]{:S(2)}, u32[]{:S(2)}) collective-permute-start(bf16[48,16,128]{2,1,0:T(8,128)(2,1)S(1)} %get-tuple-element.18), channel_id=1, source_target_pairs={{0,16},{16,32},{32,48},{48,64},{64,80},{80,96},{96,112},{112,128},... | collective-permute-start | bytes 589832 | tf_op jit(solution)/shard_map/ppermute | solution.py:378
  19.2 12.7 %collective-permute-start.3 = (bf16[45,16,128]{2,1,0:T(8,128)(2,1)S(1)}, bf16[45,16,128]{2,1,0:T(8,128)(2,1)S(1)}, u32[]{:S(2)}, u32[]{:S(2)}) collective-permute-start(bf16[45,16,128]{2,1,0:T(8,128)(2,1)S(1)} %get-tuple-element.19.low_ref), channel_id=1, source_target_pairs={{16,0},{32,16},{48,32},{64,48},{80,64},{96,80},{112,96},{128,112},... | collective-permute-start | bytes 552968 | tf_op jit(solution)/shard_map/ppermute | solution.py:378
  24.9 11.6 %copy-start.7 = (f32[4]{0:T(128)S(1)}, f32[4]{0:T(128)}, u32[]{:S(2)}) copy-start(f32[4]{0:T(128)} %param.15) | copy-start | bytes 52
  24.9 11.6 %copy-start.8 = (f32[4]{0:T(128)S(1)}, f32[4]{0:T(128)}, u32[]{:S(2)}) copy-start(f32[4]{0:T(128)} %param.14) | copy-start | bytes 52
  24.9 11.6 %copy-start.9 = (f32[4]{0:T(128)S(1)}, f32[4]{0:T(128)}, u32[]{:S(2)}) copy-start(f32[4]{0:T(128)} %param.13) | copy-start | bytes 52
  32.1 10.8 %collective-permute-start.4 = (bf16[13,13,8,128]{3,2,1,0:T(8,128)(2,1)S(1)}, bf16[13,13,8,128]{3,2,1,0:T(8,128)(2,1)S(1)}, u32[]{:S(2)}, u32[]{:S(2)}) collective-permute-start(bf16[13,13,8,128]{3,2,1,0:T(8,128)(2,1)S(1)} %get-tuple-element.24), channel_id=1, source_target_pairs={{0,4},{4,8},{8,12},{1,5},{5,9},{9,13},{2,6},{6,10},{10,14},{3,7},{... | collective-permute-start | bytes 1038344 | tf_op jit(solution)/shard_map/ppermute | solution.py:378
  35.2 11.5 %collective-permute-start.5 = (bf16[13,13,8,128]{3,2,1,0:T(8,128)(2,1)S(1)}, bf16[13,13,8,128]{3,2,1,0:T(8,128)(2,1)S(1)}, u32[]{:S(2)}, u32[]{:S(2)}) collective-permute-start(bf16[13,13,8,128]{3,2,1,0:T(8,128)(2,1)S(1)} %get-tuple-element.21.low_ref), channel_id=1, source_target_pairs={{4,0},{8,4},{12,8},{5,1},{9,5},{13,9},{6,2},{10,6},{14,10},{7,3},{... | collective-permute-start | bytes 1038344 | tf_op jit(solution)/shard_map/ppermute | solution.py:378

commit v4 on v3

--- a/solution.py
+++ b/solution.py
@@ -416,7 +416,7 @@
     )(own, before, after)
     left, right = shift(high, "gx", 1), shift(low, "gx", -1)
     u = directions(dir_angles, dir_order, low)
-    table, weight = tables(u, ints, low)
+    half = tables(u, ints, low, 0)
     low, high = pl.pallas_call(
         pack_y_kernel,
         out_shape=(jax.ShapeDtypeStruct((13, 13, 8, 128), HALO),) * 2,
@@ -424,7 +424,8 @@
         out_specs=(whole(),) * 2,
         compiler_params=kernel_options(6),
         name="pack_y",
-    )(own, before, after, left, right, weight)
+    )(own, before, after, left, right, half[1])
+    table, weight = tables(u, ints, low, 16, half)
     laid, laid_coef = pl.pallas_call(
         lay_kernel,
         out_shape=(
@@ -497,7 +498,7 @@
         return polar, azim
 
     zero = jnp.zeros(idx.shape, jnp.float32)
-    polar, azim = lax.fori_loop(0, 64, body, (zero, zero), unroll=4)
+    polar, azim = lax.fori_loop(0, 64, body, (zero, zero), unroll=16)
     cos_p, sin_p = cos_sin(polar * (1.0 / TWO_PI))
     cos_a, sin_a = cos_sin(azim * (1.0 / TWO_PI))
     u_ref[0] = sin_p * cos_a
@@ -518,7 +519,9 @@
     )(dir_angles.reshape(2, 64, 128), order, low)
 
 
-def tables_kernel(ints_ref, low_ref, u_ref, table_ref, weight_ref, pos_ref):
+def tables_kernel(first, ints_ref, low_ref, u_ref, *refs):
+    table_ref, weight_ref, pos_ref = refs[-3:]
+
     @pl.when(pl.program_id(0) == 0)
     def _():
         gx, gy, gz = ints_ref[76], ints_ref[77], ints_ref[78]
@@ -528,7 +531,7 @@
             for axis, start in enumerate((gx * 16 + (p >> 1), gy * 16 + (p & 1) * 8, gz * 128)):
                 pos_ref[axis, t : t + 1, :] = jnp.full((1, 256), start.astype(jnp.float32))
 
-    j2 = pl.multiple_of(pl.program_id(0) * 2, 2)
+    j2 = pl.multiple_of((pl.program_id(0) + first) * 2, 2)
 
     def row(axis):
         return jnp.concatenate(
@@ -565,28 +568,27 @@
         weight_ref[0, 1, 24 * g : 24 * g + 24, :] = tile_s * gc + tile_c * gs
 
 
-def tables(u, ints, low):
+def tables(u, ints, low, first, filled=()):
+    anywhere = pl.BlockSpec(memory_space=pl.ANY)
     return pl.pallas_call(
-        tables_kernel,
-        grid=(32,),
+        functools.partial(tables_kernel, first),
+        grid=(16,),
         out_shape=(
             jax.ShapeDtypeStruct((32, 512, 256), jnp.bfloat16),
             jax.ShapeDtypeStruct((32, 2, 104, 256), jnp.float32),
         ),
-        in_specs=[
-            scalars(),
-            pl.BlockSpec(memory_space=pl.ANY),
-            pl.BlockSpec((3, 64, 128), lambda j: (0, 0, 0)),
-        ],
+        in_specs=[scalars(), anywhere, pl.BlockSpec((3, 64, 128), lambda j: (0, 0, 0))]
+        + [anywhere] * len(filled),
         out_specs=(
-            pl.BlockSpec((1, 512, 256), lambda j: (j, 0, 0)),
-            pl.BlockSpec((1, 2, 104, 256), lambda j: (j, 0, 0, 0)),
+            pl.BlockSpec((1, 512, 256), lambda j: (j + first, 0, 0)),
+            pl.BlockSpec((1, 2, 104, 256), lambda j: (j + first, 0, 0, 0)),
         ),
+        input_output_aliases={3 + k: k for k in range(len(filled))},
         scratch_shapes=[pltpu.VMEM((3, 24, 256), jnp.float32)],
-        cost_estimate=pl.CostEstimate(flops=60000000, bytes_accessed=14000000, transcendentals=0),
+        cost_estimate=pl.CostEstimate(flops=30000000, bytes_accessed=7000000, transcendentals=0),
         compiler_params=kernel_options(12),
         name="tables",
-    )(ints, low, u)
+    )(ints, low, u, *filled)
 
 
 def far_kernel(scale, cur_ref, table_ref, weight_ref, out_ref, lhs_ref, acc_ref, rows_ref):

time: 86.9 us -> 84 us (0.967)
  blocking collectives: 26.4 us -> 23.6 us
    all_to_all x1, blocking collectives: 26.4 us -> 23.6 us  [shards(): received = lax.all_to_all(partial, AXES, 0, 0, tiled=True)]
    pallas_call x1 -> x2, Pallas kernels: 6.67 us -> 7.28 us  [tables(): pl.pallas_call(functools.partial(tables_kernel, first), grid=(16,), out_s...]
where the time goes in v4:
time: 84 us; the launch traced here: 83.6 us
  Pallas kernels  28.9 us (34%)
  blocking collectives  23.6 us (28%)
  starting transfers between devices  17.5 us (21%)
  waiting for transfers between devices  9.15 us (11%)
  local copies, waits for them, and re-layouts  3.54 us (4%)
  between operations  0.89 us (1%)
    all_to_all x1, blocking collectives, shards(): received = lax.all_to_all(partial, AXES, 0, 0, tiled=True)  23.6 us
    ppermute x6, starting transfers between devices, shift(): return lax.ppermute(block, axis, pairs)  17.5 us
    ppermute x6, waiting for transfers between devices, shift(): return lax.ppermute(block, axis, pairs)  9.15 us
    pallas_call x2, Pallas kernels, tables(): pl.pallas_call(functools.partial(tables_kernel, first), grid=(16,), out_s...  7.28 us
    pallas_call x1, Pallas kernels, window(): pl.pallas_call(functools.partial(window_kernel, sizes), out_shape=(jax.Sh...  6.39 us
    pallas_call x1, Pallas kernels, far_products(): pl.pallas_call(functools.partial(far_kernel, scale), grid=(32 // PER_STEP...  5.99 us
    pallas_call x1, Pallas kernels, directions(): pl.pallas_call(dirs_kernel, out_shape=jax.ShapeDtypeStruct((3, 64, 128),...  3.24 us
    unnamed x21, local copies, waits for them, and re-layouts  3.21 us
  transfers between devices with their start and end apart: 6, of which 4 were waited for; matrix products, arithmetic and copies ran while one was open for 0% of the time, Pallas kernels for 15%

profile of v4, /device:TPU:1, one launch (start us, length us, event | category | flops | bytes accessed | tf_op | source)
XLA Modules:
  0.0 83.6 jit_solution(4308027798804215294)
XLA Ops:
  0.6 0.0 copy-start.5
  0.6 0.0 copy-start.3
  0.7 0.0 copy-start.4
  0.7 0.0 copy-start.6
  0.7 2.8 %pack_depth.1 = bf16[13,16,128]{2,1,0:T(8,128)(2,1)} custom-call(f32[6,16,16,128]{3,2,1,0:T(8,128)} %fields_ref.2, f32[6,16,16,128]{3,2,1,0:T(8,128)} %pol_ref.2, s32[16,16,128]{2,1,0:T(8,128)} %mat_ref.2), custom_call_target="tpu_custom_call" | custom-call | tf_op jit(solution)/shard_map/pack_depth/pallas_call | solution.py:383
  3.5 4.9 %collective-permute-start = (bf16[13,16,128]{2,1,0:T(8,128)(2,1)}, bf16[13,16,128]{2,1,0:T(8,128)(2,1)S(1)}, u32[]{:S(2)}, u32[]{:S(2)}) collective-permute-start(bf16[13,16,128]{2,1,0:T(8,128)(2,1)} %pack_depth.1), channel_id=1, source_target_pairs={{0,1},{1,2},{2,3},{4,5},{5,6},{6,7},{8,9},{9,10},{10,11},{12,13},{... | collective-permute-start | bytes 159752 | tf_op jit(solution)/shard_map/ppermute | solution.py:378
  8.4 1.9 %collective-permute-start.1 = (bf16[13,16,128]{2,1,0:T(8,128)(2,1)}, bf16[13,16,128]{2,1,0:T(8,128)(2,1)S(1)}, u32[]{:S(2)}, u32[]{:S(2)}) collective-permute-start(bf16[13,16,128]{2,1,0:T(8,128)(2,1)} %pack_depth.1), channel_id=1, source_target_pairs={{1,0},{2,1},{3,2},{5,4},{6,5},{7,6},{9,8},{10,9},{11,10},{13,12},{... | collective-permute-start | bytes 159752 | tf_op jit(solution)/shard_map/ppermute | solution.py:378
  10.4 0.0 copy-start
  10.4 1.1 %copy-done = f32[6,16,16,128]{3,2,1,0:T(8,128)S(1)} copy-done((f32[6,16,16,128]{3,2,1,0:T(8,128)S(1)}, f32[6,16,16,128]{3,2,1,0:T(8,128)}, u32[]{:S(2)}) %copy-start) | copy-done | bytes 786456
  11.5 0.0 copy-start.1
  11.5 1.1 %copy-done.1 = f32[6,16,16,128]{3,2,1,0:T(8,128)S(1)} copy-done((f32[6,16,16,128]{3,2,1,0:T(8,128)S(1)}, f32[6,16,16,128]{3,2,1,0:T(8,128)}, u32[]{:S(2)}) %copy-start.1) | copy-done | bytes 786456
  12.6 0.9 %copy-done.2 = s32[16,16,128]{2,1,0:T(8,128)S(1)} copy-done((s32[16,16,128]{2,1,0:T(8,128)S(1)}, s32[16,16,128]{2,1,0:T(8,128)}, u32[]{:S(2)}) %copy-start.2) | copy-done | bytes 131096
  13.5 0.1 stage.1.own_ref
  13.7 0.0 copy-start.7
  13.7 0.0 copy-start.8
  13.7 0.0 copy-start.9
  13.7 0.0 collective-permute-done.before_ref
  13.7 0.4 collective-permute-done.1.after_ref
  14.1 0.2 pack_x.1
  14.3 4.9 %collective-permute-start.2 = (bf16[48,16,128]{2,1,0:T(8,128)(2,1)S(1)}, bf16[48,16,128]{2,1,0:T(8,128)(2,1)S(1)}, u32[]{:S(2)}, u32[]{:S(2)}) collective-permute-start(bf16[48,16,128]{2,1,0:T(8,128)(2,1)S(1)} %get-tuple-element.20), channel_id=1, source_target_pairs={{0,16},{16,32},{32,48},{48,64},{64,80},{80,96},{96,112},{112,128},... | collective-permute-start | bytes 589832 | tf_op jit(solution)/shard_map/ppermute | solution.py:378
  19.2 1.3 %collective-permute-start.3 = (bf16[45,16,128]{2,1,0:T(8,128)(2,1)S(1)}, bf16[45,16,128]{2,1,0:T(8,128)(2,1)S(1)}, u32[]{:S(2)}, u32[]{:S(2)}) collective-permute-start(bf16[45,16,128]{2,1,0:T(8,128)(2,1)S(1)} %get-tuple-element.21.low_ref), channel_id=1, source_target_pairs={{16,0},{32,16},{48,32},{64,48},{80,64},{96,80},{112,96},{128,112},... | collective-permute-start | bytes 552968 | tf_op jit(solution)/shard_map/ppermute | solution.py:378
  20.5 0.0 copy-done.5
  20.5 0.1 reshape.21
  20.6 0.0 copy-done.3
  20.6 0.0 copy-done.4
  20.6 0.1 reshape.24
  20.7 0.1 copy.14
  20.8 0.0 copy-done.6
  20.8 0.1 concatenate.6.ints_ref
  20.9 3.2 %dirs.1.u_ref = f32[3,64,128]{2,1,0:T(8,128)S(1)} custom-call(f32[2,64,128]{2,1,0:T(8,128)S(1)} %bitcast.13, s32[64,128]{1,0:T(8,128)S(1)} %reshape.25.order_ref, bf16[45,16,128]{2,1,0:T(8,128)(2,1)S(1)} %get-tuple-element.21.low_ref), custom_call_target="tpu_custom_call" | custom-call | flops 3000000 | bytes 300000 | tf_op jit(solution)/shard_map/dirs/pallas_call | solution.py:511
  24.1 3.6 %tables.2 = (bf16[32,512,256]{2,1,0:T(8,128)(2,1)S(1)}, f32[32,2,104,256]{3,2,1,0:T(8,128)S(1)}) custom-call(s32[79]{0:T(128)S(1)} %concatenate.6.ints_ref, bf16[45,16,128]{2,1,0:T(8,128)(2,1)S(1)} %get-tuple-element.21.low_ref, f32[3,64,128]{2,1,0:T(8,128)S(1)} %dirs.1.u_ref), custom_call_target="tpu_custom_call" | custom-call | flops 30000000 | bytes 7000000 | tf_op jit(solution)/shard_map/tables/pallas_call | solution.py:573
  27.8 4.1 %collective-permute-done.3.right_ref = bf16[45,16,128]{2,1,0:T(8,128)(2,1)S(1)} collective-permute-done((bf16[45,16,128]{2,1,0:T(8,128)(2,1)S(1)}, bf16[45,16,128]{2,1,0:T(8,128)(2,1)S(1)}, u32[]{:S(2)}, u32[]{:S(2)}) %collective-permute-start.3) | collective-permute-done | bytes 184352 | tf_op jit(solution)/shard_map/ppermute | solution.py:378
  31.9 0.0 collective-permute-done.2.left_ref
  31.9 0.2 pack_y.1
  32.1 3.1 %collective-permute-start.4 = (bf16[13,13,8,128]{3,2,1,0:T(8,128)(2,1)S(1)}, bf16[13,13,8,128]{3,2,1,0:T(8,128)(2,1)S(1)}, u32[]{:S(2)}, u32[]{:S(2)}) collective-permute-start(bf16[13,13,8,128]{3,2,1,0:T(8,128)(2,1)S(1)} %get-tuple-element.26), channel_id=1, source_target_pairs={{0,4},{4,8},{8,12},{1,5},{5,9},{9,13},{2,6},{6,10},{10,14},{3,7},{... | collective-permute-start | bytes 1038344 | tf_op jit(solution)/shard_map/ppermute | solution.py:378
  35.3 1.3 %collective-permute-start.5 = (bf16[13,13,8,128]{3,2,1,0:T(8,128)(2,1)S(1)}, bf16[13,13,8,128]{3,2,1,0:T(8,128)(2,1)S(1)}, u32[]{:S(2)}, u32[]{:S(2)}) collective-permute-start(bf16[13,13,8,128]{3,2,1,0:T(8,128)(2,1)S(1)} %get-tuple-element.23.low_ref), channel_id=1, source_target_pairs={{4,0},{8,4},{12,8},{5,1},{9,5},{13,9},{6,2},{10,6},{14,10},{7,3},{... | collective-permute-start | bytes 1038344 | tf_op jit(solution)/shard_map/ppermute | solution.py:378
  36.6 0.0 copy-done.7
  36.6 0.0 copy-done.8
  36.6 0.0 copy-done.9
  36.6 0.1 pad_maximum_fusion.medium_ref
  36.7 1.8 %lay.1 = (f32[12,24,16,256]{3,2,1,0:T(8,128)S(1)}, f32[4,24,16,256]{3,2,1,0:T(8,128)S(1)}) custom-call(f32[12]{0:T(128)S(1)} %pad_maximum_fusion.medium_ref, f32[13,16,16,128]{3,2,1,0:T(8,128)S(1)} %stage.1.own_ref, bf16[13,16,128]{2,1,0:T(8,128)(2,1)S(1)} %collective-permute-done.before_ref, bf16[13,16,128]{2,1,0:T(8,128)(2,1)S(1)} %collective-permute-done.1.after_ref, ...), custom_call_target="tpu_custom_call" | custom-call | flops 8000000 | bytes 9000000 | tf_op jit(solution)/shard_map/lay/pallas_call | solution.py:429
  38.5 3.6 %tables.3 = (bf16[32,512,256]{2,1,0:T(8,128)(2,1)S(1)}, f32[32,2,104,256]{3,2,1,0:T(8,128)S(1)}) custom-call(s32[79]{0:T(128)S(1)} %concatenate.6.ints_ref, bf16[13,13,8,128]{3,2,1,0:T(8,128)(2,1)S(1)} %get-tuple-element.23.low_ref, f32[3,64,128]{2,1,0:T(8,128)S(1)} %dirs.1.u_ref, ...), custom_call_target="tpu_custom_call", output_to_operand_aliasing={{0}: (3, {}), {1}: (4, {})} | custom-call | flops 30000000 | bytes 7000000 | tf_op jit(solution)/shard_map/tables/pallas_call | solution.py:573
  42.1 0.8 collective-permute-done.4.down_ref
  42.9 3.9 %collective-permute-done.5.up_ref = bf16[13,13,8,128]{3,2,1,0:T(8,128)(2,1)S(1)} collective-permute-done((bf16[13,13,8,128]{3,2,1,0:T(8,128)(2,1)S(1)}, bf16[13,13,8,128]{3,2,1,0:T(8,128)(2,1)S(1)}, u32[]{:S(2)}, u32[]{:S(2)}) %collective-permute-start.5) | collective-permute-done | bytes 346144 | tf_op jit(solution)/shard_map/ppermute | solution.py:378
  46.7 6.4 %window.1 = (f32[6,16,16,128]{3,2,1,0:T(8,128)}, f32[1152,128]{1,0:T(8,128)S(1)}) custom-call(s32[79]{0:T(128)S(1)} %concatenate.6.ints_ref, f32[12]{0:T(128)S(1)} %pad_maximum_fusion.medium_ref, f32[12,24,16,256]{3,2,1,0:T(8,128)S(1)} %get-tuple-element.24.laid_ref, f32[4,24,16,256]{3,2,1,0:T(8,128)S(1)} %get-tuple-element.25.laid_coef_ref, ...), custom_call_target="tpu_custom_call" | custom-call | tf_op jit(solution)/shard_map/window/pallas_call | solution.py:442
  53.1 6.0 %far.1 = bf16[512,128]{1,0:T(8,128)(2,1)S(1)} custom-call(f32[1152,128]{1,0:T(8,128)S(1)} %get-tuple-element.28.cur_ref, bf16[32,512,256]{2,1,0:T(8,128)(2,1)S(1)} %get-tuple-element.30.table_ref, f32[32,2,104,256]{3,2,1,0:T(8,128)S(1)} %get-tuple-element.31.weight_ref), custom_call_target="tpu_custom_call" | custom-call | flops 5000000000 | bytes 15000000 | tf_op jit(solution)/shard_map/far/pallas_call | solution.py:634
  59.1 23.6 %all_to_all.11 = bf16[256,2,128]{2,1,0:T(2,128)(2,1)S(1)} all-to-all(bf16[256,2,128]{2,1,0:T(2,128)(2,1)S(1)} %bitcast.14), channel_id=1, replica_groups=mesh['gx'=16,'gy'=4,'gz'=4] {'gx','gy','gz'}, dimensions={0} | all-to-all | bytes 262144 | tf_op jit(solution)/shard_map/all_to_all | solution.py:706
  82.7 0.9 %sum_sources.1 = f32[8,32]{1,0:T(8,128)} custom-call(bf16[512,128]{1,0:T(8,128)(2,1)S(1)} %bitcast.12), custom_call_target="tpu_custom_call" | custom-call | tf_op jit(solution)/shard_map/sum_sources/pallas_call | solution.py:674
  (3 shorter events, 0.0 us)
Async XLA Ops:
  0.6 19.9 %copy-start.5 = (s32[1,4,18]{2,1,0:T(4,128)S(1)}, s32[1,4,18]{2,1,0:T(4,128)}, u32[]{:S(2)}) copy-start(s32[1,4,18]{2,1,0:T(4,128)} %param.17) | copy-start | bytes 868
  0.6 20.0 %copy-start.3 = (f32[2,8192]{1,0:T(2,128)S(1)}, f32[2,8192]{1,0:T(2,128)}, u32[]{:S(2)}) copy-start(f32[2,8192]{1,0:T(2,128)} %param.18) | copy-start | bytes 196612
  0.7 20.0 %copy-start.4 = (s32[8192]{0:T(1024)S(1)}, s32[8192]{0:T(1024)}, u32[]{:S(2)}) copy-start(s32[8192]{0:T(1024)} %param.19) | copy-start | bytes 98308
  0.7 20.1 %copy-start.6 = (s32[1,4]{1,0:T(1,128)S(1)}, s32[1,4]{1,0:T(1,128)}, u32[]{:S(2)}) copy-start(s32[1,4]{1,0:T(1,128)} %param.16) | copy-start | bytes 52
  3.5 10.2 %collective-permute-start = (bf16[13,16,128]{2,1,0:T(8,128)(2,1)}, bf16[13,16,128]{2,1,0:T(8,128)(2,1)S(1)}, u32[]{:S(2)}, u32[]{:S(2)}) collective-permute-start(bf16[13,16,128]{2,1,0:T(8,128)(2,1)} %pack_depth.1), channel_id=1, source_target_pairs={{0,1},{1,2},{2,3},{4,5},{5,6},{6,7},{8,9},{9,10},{10,11},{12,13},{... | collective-permute-start | bytes 159752 | tf_op jit(solution)/shard_map/ppermute | solution.py:378
  8.4 5.7 %collective-permute-start.1 = (bf16[13,16,128]{2,1,0:T(8,128)(2,1)}, bf16[13,16,128]{2,1,0:T(8,128)(2,1)S(1)}, u32[]{:S(2)}, u32[]{:S(2)}) collective-permute-start(bf16[13,16,128]{2,1,0:T(8,128)(2,1)} %pack_depth.1), channel_id=1, source_target_pairs={{1,0},{2,1},{3,2},{5,4},{6,5},{7,6},{9,8},{10,9},{11,10},{13,12},{... | collective-permute-start | bytes 159752 | tf_op jit(solution)/shard_map/ppermute | solution.py:378
  10.4 1.1 %copy-start = (f32[6,16,16,128]{3,2,1,0:T(8,128)S(1)}, f32[6,16,16,128]{3,2,1,0:T(8,128)}, u32[]{:S(2)}) copy-start(f32[6,16,16,128]{3,2,1,0:T(8,128)} %fields_ref.2) | copy-start | bytes 2359300
  11.5 1.1 %copy-start.1 = (f32[6,16,16,128]{3,2,1,0:T(8,128)S(1)}, f32[6,16,16,128]{3,2,1,0:T(8,128)}, u32[]{:S(2)}) copy-start(f32[6,16,16,128]{3,2,1,0:T(8,128)} %pol_ref.2) | copy-start | bytes 2359300
  12.6 0.9 %copy-start.2 = (s32[16,16,128]{2,1,0:T(8,128)S(1)}, s32[16,16,128]{2,1,0:T(8,128)}, u32[]{:S(2)}) copy-start(s32[16,16,128]{2,1,0:T(8,128)} %mat_ref.2) | copy-start | bytes 393220
  13.7 22.9 %copy-start.7 = (f32[4]{0:T(128)S(1)}, f32[4]{0:T(128)}, u32[]{:S(2)}) copy-start(f32[4]{0:T(128)} %param.15) | copy-start | bytes 52
  13.7 22.9 %copy-start.8 = (f32[4]{0:T(128)S(1)}, f32[4]{0:T(128)}, u32[]{:S(2)}) copy-start(f32[4]{0:T(128)} %param.14) | copy-start | bytes 52
  13.7 22.9 %copy-start.9 = (f32[4]{0:T(128)S(1)}, f32[4]{0:T(128)}, u32[]{:S(2)}) copy-start(f32[4]{0:T(128)} %param.13) | copy-start | bytes 52
  14.3 17.6 %collective-permute-start.2 = (bf16[48,16,128]{2,1,0:T(8,128)(2,1)S(1)}, bf16[48,16,128]{2,1,0:T(8,128)(2,1)S(1)}, u32[]{:S(2)}, u32[]{:S(2)}) collective-permute-start(bf16[48,16,128]{2,1,0:T(8,128)(2,1)S(1)} %get-tuple-element.20), channel_id=1, source_target_pairs={{0,16},{16,32},{32,48},{48,64},{64,80},{80,96},{96,112},{112,128},... | collective-permute-start | bytes 589832 | tf_op jit(solution)/shard_map/ppermute | solution.py:378
  19.2 12.7 %collective-permute-start.3 = (bf16[45,16,128]{2,1,0:T(8,128)(2,1)S(1)}, bf16[45,16,128]{2,1,0:T(8,128)(2,1)S(1)}, u32[]{:S(2)}, u32[]{:S(2)}) collective-permute-start(bf16[45,16,128]{2,1,0:T(8,128)(2,1)S(1)} %get-tuple-element.21.low_ref), channel_id=1, source_target_pairs={{16,0},{32,16},{48,32},{64,48},{80,64},{96,80},{112,96},{128,112},... | collective-permute-start | bytes 552968 | tf_op jit(solution)/shard_map/ppermute | solution.py:378
  32.1 10.8 %collective-permute-start.4 = (bf16[13,13,8,128]{3,2,1,0:T(8,128)(2,1)S(1)}, bf16[13,13,8,128]{3,2,1,0:T(8,128)(2,1)S(1)}, u32[]{:S(2)}, u32[]{:S(2)}) collective-permute-start(bf16[13,13,8,128]{3,2,1,0:T(8,128)(2,1)S(1)} %get-tuple-element.26), channel_id=1, source_target_pairs={{0,4},{4,8},{8,12},{1,5},{5,9},{9,13},{2,6},{6,10},{10,14},{3,7},{... | collective-permute-start | bytes 1038344 | tf_op jit(solution)/shard_map/ppermute | solution.py:378
  35.3 11.5 %collective-permute-start.5 = (bf16[13,13,8,128]{3,2,1,0:T(8,128)(2,1)S(1)}, bf16[13,13,8,128]{3,2,1,0:T(8,128)(2,1)S(1)}, u32[]{:S(2)}, u32[]{:S(2)}) collective-permute-start(bf16[13,13,8,128]{3,2,1,0:T(8,128)(2,1)S(1)} %get-tuple-element.23.low_ref), channel_id=1, source_target_pairs={{4,0},{8,4},{12,8},{5,1},{9,5},{13,9},{6,2},{10,6},{14,10},{7,3},{... | collective-permute-start | bytes 1038344 | tf_op jit(solution)/shard_map/ppermute | solution.py:378
